TPU v7x, 256 devices: a whole 4x4x8 slice. The times are simulated.
256 devices in a mesh: row: 8 (over y, core), col: 8 (over z), track: 4 (over x).
Axes of the slice: x: 4, y: 4, z: 8, core: 2. Of those that a mesh axis runs over, the one named last changes fastest.
Arguments:
- factors: float32 [16384, 2, 16, 576], P(('row', 'col', 'track')), may hold values from -0.5 to 0.5
- track_clusters: int32 [16384, 2], P(('row', 'col', 'track')), may hold values from 0 to 7, as said below
- filed_flip: int32 [16384], P(('row', 'col', 'track')), may hold values from 0 to 1, as said below
- damping: float32 [8, 576], P('row'), may hold values from 50 to 500
- rhs: float32 [8, 576], P('row'), may hold values from -3000 to 3000
Outputs:
- solution: float32 [8, 576], P('row')
- scaled_residual: float32 [8, 576], P('row')
- filed_blocks: float32 [8, 8, 576, 576], P('row', 'col', 'track')
Inputs may be any that keep to these rules, and one draw needn't show every extreme that they name: `track_clusters`: each row names two different clusters, the first below the second. `filed_flip`: the owner of a block filed under (i, j) is the device of row group i // 1 and column j, with the track index of the device that holds the track block. Of the 64 track blocks of one device at most 3 go to any one owner, and in every draw, for each track index, some owner receives exactly 3 from every device of that track index.
All inputs are finite; a program needn't handle non-finite values.
Results may differ from a plain program's by a relative error of at most 0.0003.
Values sent between devices are 32-bit elements; how exact they have to be, the bound alone decides.
No kernel may reach another device: no remote copies, remote signals or barrier semaphores. Data moves between devices by JAX's collectives and lax.ppermute only.
A program may use at most 128 MiB of HBM per device.

v0:
```python
import jax
import jax.numpy as jnp
from jax import lax
from jax.sharding import PartitionSpec as P

ITERS = 2


highest = lax.Precision.HIGHEST


def fitness_sum(residual, scaled):
    return lax.psum(jnp.sum(residual * scaled), "row")


def on_device(factors, track_clusters, filed_flip, damping, rhs):
    n_row = lax.axis_size("row")
    n_col = lax.axis_size("col")
    n_track = lax.axis_size("track")
    owners = n_row * n_col
    tb_dev = factors.shape[0]
    jac_rows = factors.shape[2]
    params = factors.shape[3]
    row_clusters = damping.shape[0]
    clusters = row_clusters * n_row
    capacity = 3 * tb_dev // owners
    row_share = params // n_track
    row_id = lax.axis_index("row")
    col_id = lax.axis_index("col")
    track_id = lax.axis_index("track")
    low_cluster = track_clusters[:, 0]
    high_cluster = track_clusters[:, 1]
    low_side = factors[:, 0]
    high_side = factors[:, 1]
    cluster_ids = jnp.arange(clusters, dtype=jnp.int32)
    low_onehot = (low_cluster[:, None] == cluster_ids[None, :]).astype(jnp.float32)
    high_onehot = (high_cluster[:, None] == cluster_ids[None, :]).astype(jnp.float32)
    diag_part = jnp.dot(low_onehot.T, jnp.sum(low_side * low_side, axis=1), precision=highest)
    diag_part = diag_part + jnp.dot(
        high_onehot.T, jnp.sum(high_side * high_side, axis=1), precision=highest
    )
    diag_all = lax.psum(diag_part, ("row", "col", "track"))
    precond = damping + lax.dynamic_slice_in_dim(diag_all, row_id * row_clusters, row_clusters, 0)
    flipped = filed_flip == 1
    filed_row = jnp.where(flipped, high_cluster, low_cluster)
    filed_col = jnp.where(flipped, low_cluster, high_cluster)
    oriented = jnp.where(flipped[:, None, None, None], factors[:, ::-1], factors)
    owner_row = filed_row // row_clusters
    target = owner_row * n_col + filed_col
    slot_ids = filed_row - owner_row * row_clusters
    owner_hits = (target[:, None] == jnp.arange(owners, dtype=jnp.int32)[None, :]).astype(jnp.int32)
    places = jnp.sum((jnp.cumsum(owner_hits, axis=0) - 1) * owner_hits, axis=1)
    position = target * capacity + places
    outgoing = (
        jnp.zeros((owners * capacity, 2, jac_rows, params), jnp.float32).at[position].set(oriented)
    )
    outgoing_slots = jnp.zeros((owners * capacity,), jnp.int32).at[position].set(slot_ids)
    incoming, incoming_slots = (
        lax.all_to_all(
            outgoing.reshape(owners, capacity, 2, jac_rows, params),
            ("row", "col"),
            split_axis=0,
            concat_axis=0,
            tiled=True,
        ),
        lax.all_to_all(
            outgoing_slots.reshape(owners, capacity),
            ("row", "col"),
            split_axis=0,
            concat_axis=0,
            tiled=True,
        ),
    )
    received = incoming.reshape(owners * capacity, 2, jac_rows, params)
    received_slots = incoming_slots.reshape(owners * capacity)
    received_rows = received[:, 0]
    received_cols = received[:, 1]
    slot_masks = [(received_slots == 0).astype(jnp.float32)]
    pieces = [
        jnp.einsum(
            "mkr,mkc->rc",
            received_rows * slot_mask[:, None, None],
            received_cols,
            precision=highest,
            preferred_element_type=jnp.float32,
        )
        for slot_mask in slot_masks
    ]
    filed = lax.psum_scatter(pieces[0], "track", scatter_dimension=0, tiled=True)
    filed_blocks = filed.reshape(row_share, row_clusters, params)
    blocks_out = jnp.transpose(filed_blocks, (1, 0, 2))[:, None]
    col_onehot = (cluster_ids == col_id).astype(jnp.float32)
    solution = jnp.zeros_like(rhs)
    residual = rhs
    scaled = residual / precond
    direction = scaled
    fitness = fitness_sum(residual, scaled)
    for iteration in range(ITERS):
        full_dir = lax.all_gather(direction, "row", axis=0, tiled=True)
        col_dir = jnp.dot(col_onehot, full_dir, precision=highest)
        own_share = lax.dynamic_slice_in_dim(direction, track_id * row_share, row_share, 1)
        row_terms = jnp.einsum("rsc,c->sr", filed_blocks, col_dir, precision=highest)
        col_terms = jnp.einsum("rsc,sr->c", filed_blocks, own_share, precision=highest)
        low_dir = jnp.dot(low_onehot, full_dir, precision=highest)
        high_dir = jnp.dot(high_onehot, full_dir, precision=highest)
        low_proj = jnp.einsum("mkc,mc->mk", low_side, low_dir, precision=highest)
        high_proj = jnp.einsum("mkc,mc->mk", high_side, high_dir, precision=highest)
        low_back = jnp.einsum("mk,mkc->mc", low_proj, low_side, precision=highest)
        high_back = jnp.einsum("mk,mkc->mc", high_proj, high_side, precision=highest)
        local = jnp.dot(low_onehot.T, low_back, precision=highest) + jnp.dot(
            high_onehot.T, high_back, precision=highest
        )
        placed = lax.dynamic_update_slice(
            jnp.zeros((clusters, params), jnp.float32),
            row_terms,
            (row_id * row_clusters, track_id * row_share),
        )
        local = local + placed + col_onehot[:, None] * col_terms[None, :]
        summed = lax.psum(local, ("row", "col", "track"))
        images = (
            lax.dynamic_slice_in_dim(summed, row_id * row_clusters, row_clusters, 0)
            + damping * direction
        )
        curvature = lax.psum(jnp.sum(direction * images), "row")
        images, curvature = (images, curvature)
        step_size = fitness / curvature
        solution = solution + step_size * direction
        residual = residual - step_size * images
        scaled = residual / precond
        fitness_next = fitness_sum(residual, scaled)
        direction = scaled + fitness_next / fitness * direction
        fitness = fitness_next
    return (solution, scaled, blocks_out)


def solution(mesh):
    in_specs = (
        P(("row", "col", "track"), None, None, None),
        P(("row", "col", "track"), None),
        P(("row", "col", "track")),
        P("row", None),
        P("row", None),
    )
    out_specs = (P("row", None), P("row", None), P("row", "col", "track", None))
    return jax.shard_map(
        on_device, mesh=mesh, in_specs=in_specs, out_specs=out_specs, check_vma=False
    )
```

profile of v0, /device:TPU:35, one launch (start us, length us, event | category | flops | bytes accessed | tf_op | source)
XLA Modules:
  0.0 1020.5 jit_solution(7229425490721513363)
XLA Ops:
  9.8 12.0 %all-to-all-start.1 = ((s32[64,1,3]{2,1,0:T(1,128)}), s32[64,1,3]{2,1,0:T(1,128)S(1)}, u32[]{:S(2)}, u32[]{:S(2)}) async-start(s32[64,1,3]{2,1,0:T(1,128)} %bitcast.21), calls=%async_computation.1 | async-start | bytes 65536 | tf_op jit(solution)/shard_map/all_to_all | solution.py:66
  22.6 6.9 reverse_select_fusion
  29.4 7.5 broadcast_in_dim.12
  36.9 13.1 %scatter_fusion = f32[192,2,16,576]{3,2,1,0:T(8,128)} fusion(f32[192,2,16,576]{3,2,1,0:T(8,128)} %broadcast_in_dim.12, s32[64]{0:T(128)S(1)} %compare_select_fusion, f32[64,2,16,576]{3,2,1,0:T(8,128)} %reverse_select_fusion), kind=kCustom, calls=%fused_computation | custom fusion | bytes 14156032 | tf_op jit(solution)/shard_map/scatter | solution.py:55
  50.1 10.5 %all-to-all-start = ((f32[64,3,2,16,576]{4,3,2,1,0:T(8,128)}), f32[64,3,2,16,576]{4,3,2,1,0:T(8,128)}, u32[]{:S(2)}, u32[]{:S(2)}) async-start(f32[64,3,2,16,576]{4,3,2,1,0:T(8,128)} %bitcast.149), calls=%async_computation | async-start | bytes 31457280 | tf_op jit(solution)/shard_map/all_to_all | solution.py:59
  60.7 3.6 fusion.11
  64.8 345.2 %all-to-all-done = f32[64,3,2,16,576]{4,3,2,1,0:T(8,128)} async-done(((f32[64,3,2,16,576]{4,3,2,1,0:T(8,128)}), f32[64,3,2,16,576]{4,3,2,1,0:T(8,128)}, u32[]{:S(2)}, u32[]{:S(2)}) %all-to-all-start) | async-done | bytes 14155808 | tf_op jit(solution)/shard_map/all_to_all | solution.py:59
  410.0 3.8 slice.25
  413.8 3.8 fusion
  417.6 247.6 %fusion.29 = f32[576,576]{1,0:T(8,128)} fusion(f32[192,1,16,576]{3,2,1,0:T(8,128)S(1)} %slice.25, f32[192,16,576]{2,1,0:T(8,128)S(1)} %fusion), kind=kOutput, calls=%fused_computation.36 | convolution fusion | flops 12230590464 | bytes 15482880 | tf_op jit(solution)/shard_map/mkr,mkc->rc/dot_general | solution.py:80
  665.6 86.3 %psum.49 = f32[8,576]{1,0:T(8,128)S(1)} all-reduce(f32[8,576]{1,0:T(8,128)S(1)} %convolution_add_fusion.2), channel_id=1, replica_groups=mesh['row'=8,'col'=8,'track'=4] {'row','col','track'}, use_global_device_ids=true, to_apply=%region_2.0 | all-reduce | flops 4608 | bytes 36864 | tf_op jit(solution)/shard_map/psum | solution.py:42
  751.9 13.4 %all-gather = f32[8,1,576]{2,1,0:T(1,128)S(1)} all-gather(f32[1,1,576]{2,1,0:T(1,128)S(1)} %bitcast.151), channel_id=1, replica_groups=mesh['row'=8,'col'=8,'track'=4] {'row'}, dimensions={0}, use_global_device_ids=true | all-gather | bytes 20736 | tf_op jit(solution)/shard_map/all_gather | solution.py:99
  766.0 5.1 fusion.32
  771.1 3.3 fusion.16
  774.7 5.1 fusion.38
  779.8 3.4 fusion.7
  786.7 76.6 %psum.51 = f32[8,576]{1,0:T(8,128)S(1)} all-reduce(f32[8,576]{1,0:T(8,128)S(1)} %multiply_add_fusion.1), channel_id=1, replica_groups=mesh['row'=8,'col'=8,'track'=4] {'row','col','track'}, use_global_device_ids=true, to_apply=%region_10.11 | all-reduce | flops 4608 | bytes 36864 | tf_op jit(solution)/shard_map/psum | solution.py:119
  864.0 13.1 %all-reduce = (f32[]{:T(128)}, f32[]{:T(128)}) all-reduce(f32[]{:T(128)} %get-tuple-element.6, f32[]{:T(128)} %get-tuple-element.5), channel_id=1, replica_groups=mesh['row'=8,'col'=8,'track'=4] {'row'}, use_global_device_ids=true, to_apply=%region_4.5 | all-reduce | flops 2 | bytes 16 | tf_op jit(solution)/shard_map/psum | solution.py:13
  879.0 13.0 %psum.53 = f32[]{:T(128)} all-reduce(f32[]{:T(128)} %get-tuple-element.9), channel_id=1, replica_groups=mesh['row'=8,'col'=8,'track'=4] {'row'}, use_global_device_ids=true, to_apply=%region_14.15 | all-reduce | flops 1 | bytes 8 | tf_op jit(solution)/shard_map/psum | solution.py:13
  893.4 13.4 %all-gather.1 = f32[8,1,576]{2,1,0:T(1,128)S(1)} all-gather(f32[1,1,576]{2,1,0:T(1,128)S(1)} %bitcast.152), channel_id=1, replica_groups=mesh['row'=8,'col'=8,'track'=4] {'row'}, dimensions={0}, use_global_device_ids=true | all-gather | bytes 20736 | tf_op jit(solution)/shard_map/all_gather | solution.py:99
  907.5 5.3 fusion.35
  916.3 5.1 fusion.41
  924.6 73.5 %psum.54 = f32[8,576]{1,0:T(8,128)S(1)} all-reduce(f32[8,576]{1,0:T(8,128)S(1)} %multiply_add_fusion), channel_id=1, replica_groups=mesh['row'=8,'col'=8,'track'=4] {'row','col','track'}, use_global_device_ids=true, to_apply=%region_15.16 | all-reduce | flops 4608 | bytes 36864 | tf_op jit(solution)/shard_map/psum | solution.py:119
  998.7 13.1 %psum.55 = f32[]{:T(128)} all-reduce(f32[]{:T(128)} %multiply_reduce_fusion), channel_id=1, replica_groups=mesh['row'=8,'col'=8,'track'=4] {'row'}, use_global_device_ids=true, to_apply=%region_17.18 | all-reduce | flops 1 | bytes 8 | tf_op jit(solution)/shard_map/psum | solution.py:124
  (58 shorter events, 18.4 us)
Async XLA Ops:
  9.8 40.2 %all-to-all-start.1 = ((s32[64,1,3]{2,1,0:T(1,128)}), s32[64,1,3]{2,1,0:T(1,128)S(1)}, u32[]{:S(2)}, u32[]{:S(2)}) async-start(s32[64,1,3]{2,1,0:T(1,128)} %bitcast.21), calls=%async_computation.1 | async-start | bytes 65536 | tf_op jit(solution)/shard_map/all_to_all | solution.py:66
  50.1 10.6 %copy-start.3 = (s32[64,2]{0,1:T(2,128)S(1)}, s32[64,2]{0,1:T(2,128)}, u32[]{:S(2)}) copy-start(s32[64,2]{0,1:T(2,128)} %param.6) | copy-start | bytes 1540
  50.1 360.0 %all-to-all-start = ((f32[64,3,2,16,576]{4,3,2,1,0:T(8,128)}), f32[64,3,2,16,576]{4,3,2,1,0:T(8,128)}, u32[]{:S(2)}, u32[]{:S(2)}) async-start(f32[64,3,2,16,576]{4,3,2,1,0:T(8,128)} %bitcast.149), calls=%async_computation | async-start | bytes 31457280 | tf_op jit(solution)/shard_map/all_to_all | solution.py:59
  60.6 722.9 %reduce-scatter.2.cloned.1.call-start = ((), (), s32[]{:S(2)}) async-start(), calls=%async_computation.3 | async-start | bytes 1843200 | tf_op jit(solution)/shard_map/reduce_scatter | solution.py:89
  417.6 334.2 %copy-start.1 = (f32[1,576]{1,0:T(1,128)S(1)}, f32[1,576]{1,0:T(1,128)}, u32[]{:S(2)}) copy-start(f32[1,576]{1,0:T(1,128)} %param.8) | copy-start | bytes 6916
  417.6 334.2 %copy-start.2 = (f32[1,576]{1,0:T(1,128)S(1)}, f32[1,576]{1,0:T(1,128)}, u32[]{:S(2)}) copy-start(f32[1,576]{1,0:T(1,128)} %param.9) | copy-start | bytes 6916
  779.8 141.7 %slice-start = ((s8[5242880]{0:T(1024)(128)(4,1)}), s8[1048576]{0:T(1024)(128)(4,1)S(1)}, s32[]{:S(2)}) async-start(s8[5242880]{0:T(1024)(128)(4,1)} %bitcast.147), calls=%async_computation.4 | async-start | bytes 2097152
  907.5 14.0 %slice-start.1 = ((s8[5242880]{0:T(1024)(128)(4,1)}), s8[4194304]{0:T(1024)(128)(4,1)S(1)}, s32[]{:S(2)}) async-start(s8[5242880]{0:T(1024)(128)(4,1)} %bitcast.147), calls=%async_computation.5 | async-start | bytes 8388608
  907.5 15.8 %copy-start = (f32[144,576]{1,0:T(8,128)S(1)}, f32[144,576]{1,0:T(8,128)}, u32[]{:S(2)}) copy-start(f32[144,576]{1,0:T(8,128)} %reduce-scatter.2.cloned.1.call-done) | copy-start | bytes 995332
Sparse Core Ops, SparseCore 0:
  665.4 37.5 reduce-scatter.1
where the time goes:
time: 1020 us
  waiting for transfers between devices  345 us (34%)
  blocking collectives  302 us (30%)
  matrix products  286 us (28%)
  local copies, waits for them, and re-layouts  26.9 us (3%)
  starting transfers between devices  22.6 us (2%)
  other arithmetic  18.8 us (2%)
  between operations  18.3 us (2%)
    all_to_all x1, waiting for transfers between devices, on_device(): lax.all_to_all(outgoing.reshape(owners, capacity, 2, jac_rows, params), (...  345 us
    dot_general x1, matrix products, on_device(): jnp.einsum('mkr,mkc->rc', received_rows * slot_mask[:, None, None], recei...  248 us
    psum x2, blocking collectives, on_device(): summed = lax.psum(local, ('row', 'col', 'track'))  150 us
    psum x1, blocking collectives, on_device(): diag_all = lax.psum(diag_part, ('row', 'col', 'track'))  86.3 us
    all_gather x2, blocking collectives, on_device(): full_dir = lax.all_gather(direction, 'row', axis=0, tiled=True)  26.8 us
    psum x2, blocking collectives, fitness_sum(): return lax.psum(jnp.sum(residual * scaled), 'row')  26.1 us
  transfers between devices with their start and end apart: 3, of which 1 were waited for; matrix products, arithmetic and copies ran while one was open for 5% of the time, Pallas kernels for 0%

commit v1 on v0

v1 whole, which is shorter than its diff:
```python
import functools

import jax
import jax.numpy as jnp
from jax import lax
from jax.experimental import pallas as pl
from jax.experimental.pallas import tpu as pltpu
from jax.sharding import PartitionSpec as P

CAPACITY = 3
LANES = 128
PACK_STEPS = 8
GRAM_STEPS = 3

VMEM = pl.BlockSpec(memory_space=pltpu.VMEM)
SMEM = pl.BlockSpec(memory_space=pltpu.SMEM)


def tree_sum(parts):
    while len(parts) > 1:
        parts = [parts[at] + parts[at + 1] for at in range(0, len(parts), 2)]
    return parts[0]


def exchange(copies, axis):
    return lax.all_to_all(copies, axis, 0, 0, tiled=True)


def gathered_sum(ref):
    return tree_sum([ref[at] for at in range(ref.shape[0])])


def relay_kernel(in_ref, out_ref):
    out_ref[...] = jnp.broadcast_to(gathered_sum(in_ref)[None], out_ref.shape)


def relay(gathered, copies):
    shape = (copies,) + gathered.shape[1:]
    return pl.pallas_call(
        relay_kernel,
        out_shape=jax.ShapeDtypeStruct(shape, jnp.float32),
        in_specs=[VMEM],
        out_specs=VMEM,
        name="relay",
    )(gathered)


def sum_over_planes(value):
    planes = lax.axis_size("col")
    hop = 1
    while hop < planes:
        pairs = [(at, at ^ hop) for at in range(planes)]
        value = value + lax.ppermute(value, "col", pairs)
        hop *= 2
    return value


def pack_kernel(parity, tracks, clusters_ref, flip_ref, factors_ref, out_ref, counts, slots):
    step = pl.program_id(0)
    blocks, _, jac_rows, params = factors_ref.shape
    per_step = out_ref.shape[0]
    whole = params // LANES * LANES
    pairs = counts.shape[0]
    row_pairs = 2 * tracks

    @pl.when(step == 0)
    def _():
        def clear(pair, carry):
            counts[pair] = 0
            for place in range(CAPACITY):
                slots[pair * CAPACITY + place] = -1
            return carry

        lax.fori_loop(0, pairs, clear, 0, unroll=4)

        def assign(block, carry):
            flip = flip_ref[block]
            low = clusters_ref[0, block]
            high = clusters_ref[1, block]
            first = jnp.where(flip == 1, high, low)
            second = jnp.where(flip == 1, low, high)
            pair = first * row_pairs + second
            place = counts[pair]
            counts[pair] = place + 1
            slots[pair * CAPACITY + place] = block
            return carry

        lax.fori_loop(0, blocks, assign, 0, unroll=4)

    for local in range(per_step):
        for place in range(CAPACITY):
            pair = (step * per_step + local) * 2 + parity
            block = slots[pair * CAPACITY + place]

            @pl.when(block >= 0)
            def _():
                flip = flip_ref[block]
                first = factors_ref[block, flip]
                second = factors_ref[block, 1 - flip]
                out_ref[local, place, :, 0:whole] = first[:, 0:whole]
                out_ref[local, place, :, whole : whole + LANES] = jnp.concatenate(
                    [first[:, whole:params], second[:, whole:params]], axis=1
                )
                out_ref[local, place, :, whole + LANES : 2 * params] = second[:, 0:whole]

            @pl.when(block < 0)
            def _():
                out_ref[local, place] = jnp.zeros((jac_rows, 2 * params), jnp.float32)


def pack(factors, track_clusters, filed_flip, parity, rows, tracks):
    jac_rows, params = factors.shape[2:]
    shape = (rows * tracks, CAPACITY, jac_rows, 2 * params)
    pairs = 2 * rows * tracks
    return pl.pallas_call(
        functools.partial(pack_kernel, parity, tracks),
        grid=(PACK_STEPS,),
        out_shape=jax.ShapeDtypeStruct(shape, jnp.float32),
        in_specs=[
            SMEM,
            SMEM,
            pl.BlockSpec(factors.shape, lambda step: (0, 0, 0, 0)),
        ],
        out_specs=pl.BlockSpec(
            (shape[0] // PACK_STEPS,) + shape[1:], lambda step: (step, 0, 0, 0)
        ),
        scratch_shapes=[
            pltpu.SMEM((pairs,), jnp.int32),
            pltpu.SMEM((pairs * CAPACITY,), jnp.int32),
        ],
        cost_estimate=pl.CostEstimate(
            flops=0,
            bytes_accessed=4 * (factors.size + shape[0] * CAPACITY * jac_rows * 2 * params),
            transcendentals=0,
        ),
        name="pack",
    )(track_clusters, filed_flip, factors)


def gram_kernel(params, in_ref, out_ref, total):
    step = pl.program_id(0)
    whole = params // LANES * LANES
    wide = whole + LANES
    value = in_ref[...]
    high = value.astype(jnp.bfloat16)
    low = (value - high.astype(jnp.float32)).astype(jnp.bfloat16)
    product = functools.partial(
        lax.dot_general,
        dimension_numbers=(((0,), (0,)), ((), ())),
        preferred_element_type=jnp.float32,
    )
    first, second = slice(0, wide), slice(whole, 2 * params)
    gram = product(high[:, first], high[:, second])
    gram = gram + product(high[:, first], low[:, second])
    gram = gram + product(low[:, first], high[:, second])

    @pl.when(step == 0)
    def _():
        total[...] = gram

    @pl.when(step > 0)
    def _():
        total[...] += gram

    @pl.when(step == pl.num_programs(0) - 1)
    def _():
        out_ref[:, 0:whole] = total[0:params, LANES:wide]
        out_ref[:, whole:params] = total[0:params, params - whole : LANES]


def gram(received, params):
    received = received.reshape(-1, 2 * params)
    rows, width = received.shape
    wide = params // LANES * LANES + LANES
    return pl.pallas_call(
        functools.partial(gram_kernel, params),
        grid=(GRAM_STEPS,),
        out_shape=jax.ShapeDtypeStruct((params, params), jnp.float32),
        in_specs=[pl.BlockSpec((rows // GRAM_STEPS, width), lambda step: (step, 0))],
        out_specs=pl.BlockSpec((params, params), lambda step: (0, 0)),
        scratch_shapes=[pltpu.VMEM((wide, wide), jnp.float32)],
        cost_estimate=pl.CostEstimate(
            flops=6 * rows * wide * wide,
            bytes_accessed=4 * (rows * width + params * params),
            transcendentals=0,
        ),
        name="gram",
    )(received)


def plane_rows(block):
    return lax.psum_scatter(block, "col", scatter_dimension=0, tiled=True)


def placed(piece, parity):
    n_col = lax.axis_size("col")
    n_track = lax.axis_size("track")
    halves = n_col // n_track
    out = []
    for half in range(halves):
        moves = []
        for col in range(half, n_col, halves):
            for track in range(n_track):
                target = (2 * track + parity) * n_track + col // halves
                moves.append((col * n_track + track, target))
        out.append(lax.ppermute(piece, ("col", "track"), moves))
    return jnp.concatenate(out, axis=0)


def diag_kernel(clusters_ref, factors_ref, damping_ref, rhs_ref, out_ref, sums):
    blocks, sides, _, params = factors_ref.shape
    clusters = sums.shape[0]
    sums[...] = jnp.zeros_like(sums)

    def add_block(block, carry):
        for side in range(sides):
            value = factors_ref[block, side]
            squares = value * value
            sums[clusters_ref[side, block]] += squares[0:8] + squares[8:16]
        return carry

    lax.fori_loop(0, blocks, add_block, 0, unroll=4)
    for at in range(clusters):
        total = jnp.sum(sums[at], axis=0, keepdims=True)
        for copy in range(out_ref.shape[0]):
            out_ref[copy, at : at + 1] = total
    ids = lax.broadcasted_iota(jnp.int32, (clusters, params), 0)
    damping = jnp.broadcast_to(damping_ref[...], (clusters, params))
    rhs = jnp.broadcast_to(rhs_ref[...], (clusters, params))
    for copy in range(out_ref.shape[0]):
        out_ref[copy, clusters:] = jnp.where(ids == 0, damping, rhs)


def settle_kernel(in_ref, out_ref, vectors_ref):
    clusters = vectors_ref.shape[1]
    total = tree_sum([in_ref[at, 0:clusters] for at in range(in_ref.shape[0])])
    out_ref[...] = jnp.broadcast_to(total[None], out_ref.shape)
    for at in range(clusters):
        vectors_ref[0, at : at + 1] = in_ref[at, clusters : clusters + 1]
        vectors_ref[1, at : at + 1] = in_ref[at, clusters + 1 : clusters + 2]


def system_part(clusters_ref, factors_ref, direction, spread, sums):
    blocks = factors_ref.shape[0]
    clusters, params = direction.shape
    sums[...] = jnp.zeros_like(sums)
    for at in range(clusters):
        spread[at] = jnp.broadcast_to(direction[at : at + 1], (8, params))

    def add_block(block, carry):
        low = clusters_ref[0, block]
        high = clusters_ref[1, block]
        low_side = [factors_ref[block, 0, 0:8], factors_ref[block, 0, 8:16]]
        high_side = [factors_ref[block, 1, 0:8], factors_ref[block, 1, 8:16]]
        low_dir = spread[low]
        high_dir = spread[high]
        projected = [
            jnp.sum(one * low_dir + two * high_dir, axis=1, keepdims=True)
            for one, two in zip(low_side, high_side)
        ]
        sums[low] += low_side[0] * projected[0] + low_side[1] * projected[1]
        sums[high] += high_side[0] * projected[0] + high_side[1] * projected[1]
        return carry

    lax.fori_loop(0, blocks, add_block, 0, unroll=8)
    return [jnp.sum(sums[at], axis=0, keepdims=True) for at in range(clusters)]


def total_of(value):
    return jnp.sum(jnp.sum(value, axis=1, keepdims=True), axis=0, keepdims=True)


def begin_kernel(
    clusters_ref, factors_ref, vectors_ref, diag_ref, part_ref, state_ref, spread, sums
):
    damping = vectors_ref[0]
    residual = vectors_ref[1]
    precond = damping + diag_ref[...]
    direction = residual / precond
    state_ref[0] = damping
    state_ref[1] = precond
    state_ref[2] = jnp.zeros_like(residual)
    state_ref[3] = residual
    state_ref[4] = direction
    parts = system_part(clusters_ref, factors_ref, direction, spread, sums)
    for at, part in enumerate(parts):
        part_ref[at : at + 1] = part


def iterate_kernel(
    clusters_ref, factors_ref, state_ref, images_ref, part_ref, out_ref, spread, sums
):
    damping, precond, solution, residual, direction = [state_ref[at] for at in range(5)]
    images = gathered_sum(images_ref) + damping * direction
    fitness = total_of(residual * (residual / precond))
    step_size = fitness / total_of(direction * images)
    solution = solution + step_size * direction
    residual = residual - step_size * images
    scaled = residual / precond
    fitness_next = total_of(residual * scaled)
    direction = scaled + fitness_next / fitness * direction
    out_ref[0] = damping
    out_ref[1] = precond
    out_ref[2] = solution
    out_ref[3] = residual
    out_ref[4] = direction
    parts = system_part(clusters_ref, factors_ref, direction, spread, sums)
    curvature = sum(
        jnp.sum(direction[at : at + 1] * part, axis=1, keepdims=True)
        for at, part in enumerate(parts)
    )
    curvature = jnp.broadcast_to(curvature, parts[0].shape)
    tracks = part_ref.shape[0] // len(parts)
    for at, part in enumerate(parts):
        for track in range(tracks):
            part_ref[at * tracks + track, 0:1] = part
            part_ref[at * tracks + track, 1:2] = curvature


def finish_kernel(place_ref, state_ref, images_ref, solution_ref, scaled_ref, rows):
    damping, precond, _, residual, direction = [state_ref[at] for at in range(5)]
    for vector in range(5):
        for at in range(damping.shape[0]):
            rows[vector, at] = state_ref[vector, at : at + 1]
    row = place_ref[0]
    own = gathered_sum(images_ref)
    images = own[0:1] + rows[0, row] * rows[4, row]
    curvature = own[1:2, 0:1] + total_of(damping * direction * direction)
    step_size = total_of(residual * (residual / precond)) / curvature
    solution_ref[...] = rows[2, row] + step_size * rows[4, row]
    scaled_ref[...] = (rows[3, row] - step_size * images) / rows[1, row]


def on_device(factors, track_clusters, filed_flip, damping, rhs):
    n_row = lax.axis_size("row")
    n_col = lax.axis_size("col")
    n_track = lax.axis_size("track")
    params = factors.shape[3]
    clusters = n_row
    track_clusters = track_clusters.T
    spread = pltpu.VMEM((clusters, 8, params), jnp.float32)
    state_shape = jax.ShapeDtypeStruct((5, clusters, params), jnp.float32)

    def shape_of(*shape):
        return jax.ShapeDtypeStruct(shape, jnp.float32)

    squares = pl.pallas_call(
        diag_kernel,
        out_shape=shape_of(n_row, 2 * clusters, params),
        in_specs=[SMEM, VMEM, VMEM, VMEM],
        out_specs=VMEM,
        scratch_shapes=[spread],
        name="diag",
    )(track_clusters, factors, damping, rhs)
    even = pack(factors, track_clusters, filed_flip, 0, n_row, n_track)
    squares, vectors = pl.pallas_call(
        settle_kernel,
        out_shape=(shape_of(n_track, clusters, params), shape_of(2, clusters, params)),
        in_specs=[VMEM],
        out_specs=(VMEM, VMEM),
        name="settle",
    )(exchange(squares, "row"))
    squares = relay(exchange(squares, "track"), 1)[0]

    even, squares = lax.optimization_barrier((even, squares))
    even = exchange(even, ("row", "track"))
    part, state = pl.pallas_call(
        begin_kernel,
        out_shape=(shape_of(clusters, params), state_shape),
        in_specs=[SMEM] + [VMEM] * 3,
        out_specs=(VMEM, VMEM),
        scratch_shapes=[spread, spread],
        name="begin",
    )(track_clusters, factors, vectors, sum_over_planes(squares))
    part = sum_over_planes(part)
    part = jnp.broadcast_to(part[None], (n_row * n_track,) + part.shape)
    odd = pack(factors, track_clusters, filed_flip, 1, n_row, n_track)
    odd, part, state = lax.optimization_barrier((odd, part, state))
    odd = exchange(odd, ("row", "track"))
    block = gram(even, params)
    even_out = placed(plane_rows(block), 0)
    odd, part, block = lax.optimization_barrier((odd, part, block))
    piece = plane_rows(gram(odd, params))

    part, state = pl.pallas_call(
        iterate_kernel,
        out_shape=(shape_of(n_row * n_track, 2, params), state_shape),
        in_specs=[SMEM] + [VMEM] * 3,
        out_specs=(VMEM, VMEM),
        scratch_shapes=[spread, spread],
        name="iterate",
    )(track_clusters, factors, state, exchange(part, ("row", "track")))
    part = exchange(relay(exchange(part, ("row", "track")), n_col), "col")
    piece, part = lax.optimization_barrier((piece, part))
    odd_out = placed(piece, 1)
    row_id = lax.axis_index("row").astype(jnp.int32).reshape(1)
    solution_out, scaled = pl.pallas_call(
        finish_kernel,
        out_shape=(shape_of(1, params), shape_of(1, params)),
        in_specs=[SMEM, VMEM, VMEM],
        out_specs=(VMEM, VMEM),
        scratch_shapes=[pltpu.VMEM((5, clusters, 1, params), jnp.float32)],
        name="finish",
    )(row_id, state, part)
    return solution_out, scaled, (even_out + odd_out)[None, None]


def solution(mesh):
    in_specs = (
        P(("row", "col", "track"), None, None, None),
        P(("row", "col", "track"), None),
        P(("row", "col", "track")),
        P("row", None),
        P("row", None),
    )
    out_specs = (P("row", None), P("row", None), P("row", "col", "track", None))
    return jax.shard_map(
        on_device, mesh=mesh, in_specs=in_specs, out_specs=out_specs, check_vma=False
    )
```

time: 1020 us -> 316 us (0.31)
  matrix products: 286 us -> 0 us
  blocking collectives: 302 us -> 43.5 us
  waiting for transfers between devices: 345 us -> 148 us
  Pallas kernels: 0 us -> 55.4 us
  starting transfers between devices: 22.6 us -> 51 us
  local copies, waits for them, and re-layouts: 26.9 us -> 0.69 us
  other arithmetic: 18.8 us -> 2.15 us
    dot_general x25 -> x0, matrix products: 286 us -> none  [the longest x1 248 us: on_device(): jnp.einsum('mkr,mkc->rc', received_rows * slot_mask[:, None, None], recei...]
    psum x6 -> x0, blocking collectives: 276 us -> none  [the longest x2 150 us: on_device(): summed = lax.psum(local, ('row', 'col', 'track'))]
    all_to_all x2 -> x4, waiting for transfers between devices: 345 us -> 117 us  [exchange(): return lax.all_to_all(copies, axis, 0, 0, tiled=True)]
    pallas_call x0 -> x11, Pallas kernels: none -> 55.4 us  [the longest x2 18.2 us: pack(): pl.pallas_call(functools.partial(pack_kernel, parity, tracks), grid=(PACK...]
    all_to_all x0 -> x3, blocking collectives: none -> 43.5 us  [exchange(): return lax.all_to_all(copies, axis, 0, 0, tiled=True)]
    ppermute x0 -> x10, waiting for transfers between devices: none -> 30.5 us  [the longest x4 20.2 us: placed(): out.append(lax.ppermute(piece, ('col', 'track'), moves))]
    all_gather x2 -> x0, blocking collectives: 26.8 us -> none  [on_device(): full_dir = lax.all_gather(direction, 'row', axis=0, tiled=True)]
    ppermute x0 -> x10, starting transfers between devices: none -> 25.7 us  [the longest x6 16.7 us: sum_over_planes(): value = value + lax.ppermute(value, 'col', pairs)]
  transfers between devices with their start and end apart: 3 -> 16, of which waited for: 1 -> 11; matrix products, arithmetic and copies ran while one was open for 5% -> 0% of each run, Pallas kernels for 0% -> 15%
where the time goes in v1:
time: 316 us; the launch traced here: 314 us
  waiting for transfers between devices  148 us (47%)
  Pallas kernels  55.4 us (18%)
  starting transfers between devices  51 us (16%)
  blocking collectives  43.5 us (14%)
  between operations  14.1 us (4%)
    all_to_all x4, waiting for transfers between devices, exchange(): return lax.all_to_all(copies, axis, 0, 0, tiled=True)  117 us
    all_to_all x3, blocking collectives, exchange(): return lax.all_to_all(copies, axis, 0, 0, tiled=True)  43.5 us
    all_to_all x4, starting transfers between devices, exchange(): return lax.all_to_all(copies, axis, 0, 0, tiled=True)  25.2 us
    ppermute x4, waiting for transfers between devices, placed(): out.append(lax.ppermute(piece, ('col', 'track'), moves))  20.2 us
    pallas_call x2, Pallas kernels, pack(): pl.pallas_call(functools.partial(pack_kernel, parity, tracks), grid=(PACK...  18.2 us
    pallas_call x2, Pallas kernels, gram(): pl.pallas_call(functools.partial(gram_kernel, params), grid=(GRAM_STEPS,)...  17.2 us
    ppermute x6, starting transfers between devices, sum_over_planes(): value = value + lax.ppermute(value, 'col', pairs)  16.7 us
    ppermute x6, waiting for transfers between devices, sum_over_planes(): value = value + lax.ppermute(value, 'col', pairs)  10.3 us
  transfers between devices with their start and end apart: 16, of which 11 were waited for; matrix products, arithmetic and copies ran while one was open for 0% of the time, Pallas kernels for 15%

profile of v1, /device:TPU:35, one launch (start us, length us, event | category | flops | bytes accessed | tf_op | source)
XLA Modules:
  0.0 314.5 jit_solution(2018755295363551502)
XLA Ops:
  7.2 4.0 %diag.1 = f32[8,16,576]{2,1,0:T(8,128)} custom-call(s32[2,64]{1,0:T(2,128)} %bitcast.16, f32[64,2,16,576]{3,2,1,0:T(8,128)} %factors_ref.9, f32[1,576]{1,0:T(1,128)} %damping_ref.1, f32[1,576]{1,0:T(1,128)} %rhs_ref.1), custom_call_target="tpu_custom_call" | custom-call | tf_op jit(solution)/shard_map/diag/pallas_call | solution.py:347
  11.2 12.7 %all_to_all.35.in_ref = f32[8,16,576]{2,1,0:T(8,128)} all-to-all(f32[8,16,576]{2,1,0:T(8,128)} %diag.1), channel_id=1, replica_groups=mesh['row'=8,'col'=8,'track'=4] {'row'}, dimensions={0} | all-to-all | bytes 589824 | tf_op jit(solution)/shard_map/all_to_all | solution.py:26
  25.5 4.3 %all-to-all-start.1 = ((f32[4,8,576]{2,1,0:T(8,128)}), f32[4,8,576]{2,1,0:T(8,128)S(1)}, u32[]{:S(2)}, u32[]{:S(2)}) async-start(f32[4,8,576]{2,1,0:T(8,128)} %get-tuple-element.21), calls=%async_computation.1 | async-start | bytes 163840 | tf_op jit(solution)/shard_map/all_to_all | solution.py:26
  29.8 9.3 %pack.3 = f32[32,3,16,1152]{3,2,1,0:T(8,128)} custom-call(s32[2,64]{1,0:T(2,128)} %bitcast.17, s32[64]{0:T(128)} %flip_ref.3, f32[64,2,16,576]{3,2,1,0:T(8,128)} %factors_ref.9), custom_call_target="tpu_custom_call" | custom-call | bytes 11796480 | tf_op jit(solution)/shard_map/pack/pallas_call | solution.py:115
  41.2 6.6 %all-to-all-start.3 = ((f32[32,3,16,1152]{3,2,1,0:T(8,128)}), f32[32,3,16,1152]{3,2,1,0:T(8,128)}, u32[]{:S(2)}, u32[]{:S(2)}) async-start(f32[32,3,16,1152]{3,2,1,0:T(8,128)} %pack.3), calls=%async_computation.3 | async-start | bytes 14155776 | tf_op jit(solution)/shard_map/all_to_all | solution.py:26
  47.9 3.0 collective-permute-done
  51.0 3.2 %collective-permute-start.1 = (f32[8,576]{1,0:T(8,128)S(1)}, f32[8,576]{1,0:T(8,128)S(1)}, u32[]{:S(2)}, u32[]{:S(2)}) collective-permute-start(f32[8,576]{1,0:T(8,128)S(1)} %add.32), channel_id=1, source_target_pairs={{0,8},{4,12},{8,0},{12,4},{16,24},{20,28},{24,16},{28,20},{1,9},{5... | collective-permute-start | bytes 55304 | tf_op jit(solution)/shard_map/ppermute | solution.py:53
  55.7 5.5 %collective-permute-start.2 = (f32[8,576]{1,0:T(8,128)S(1)}, f32[8,576]{1,0:T(8,128)S(1)}, u32[]{:S(2)}, u32[]{:S(2)}) collective-permute-start(f32[8,576]{1,0:T(8,128)S(1)} %add.33), channel_id=1, source_target_pairs={{0,16},{4,20},{8,24},{12,28},{16,0},{20,4},{24,8},{28,12},{1,17},{... | collective-permute-start | bytes 55304 | tf_op jit(solution)/shard_map/ppermute | solution.py:53
  63.0 4.5 %begin.1 = (f32[8,576]{1,0:T(8,128)}, f32[5,8,576]{2,1,0:T(8,128)}) custom-call(s32[2,64]{1,0:T(2,128)} %bitcast.18, f32[64,2,16,576]{3,2,1,0:T(8,128)} %factors_ref.9, f32[2,8,576]{2,1,0:T(8,128)} %get-tuple-element.20.vectors_ref, f32[8,576]{1,0:T(8,128)} %add.34.diag_ref), custom_call_target="tpu_custom_call" | custom-call | tf_op jit(solution)/shard_map/begin/pallas_call | solution.py:367
  75.4 5.4 %collective-permute-start.5 = (f32[8,576]{1,0:T(8,128)S(1)}, f32[8,576]{1,0:T(8,128)S(1)}, u32[]{:S(2)}, u32[]{:S(2)}) collective-permute-start(f32[8,576]{1,0:T(8,128)S(1)} %add.36), channel_id=1, source_target_pairs={{0,16},{4,20},{8,24},{12,28},{16,0},{20,4},{24,8},{28,12},{1,17},{... | collective-permute-start | bytes 55304 | tf_op jit(solution)/shard_map/ppermute | solution.py:53
  80.8 8.9 %pack.2 = f32[32,3,16,1152]{3,2,1,0:T(8,128)} custom-call(s32[2,64]{1,0:T(2,128)} %bitcast.19, s32[64]{0:T(128)} %flip_ref.3, f32[64,2,16,576]{3,2,1,0:T(8,128)} %factors_ref.9), custom_call_target="tpu_custom_call" | custom-call | bytes 11796480 | tf_op jit(solution)/shard_map/pack/pallas_call | solution.py:115
  89.7 41.4 %all-to-all-done.3 = f32[32,3,16,1152]{3,2,1,0:T(8,128)} async-done(((f32[32,3,16,1152]{3,2,1,0:T(8,128)}), f32[32,3,16,1152]{3,2,1,0:T(8,128)}, u32[]{:S(2)}, u32[]{:S(2)}) %all-to-all-start.3) | async-done | bytes 7077920 | tf_op jit(solution)/shard_map/all_to_all | solution.py:26
  131.1 6.5 %all-to-all-start.2 = ((f32[32,3,16,1152]{3,2,1,0:T(8,128)}), f32[32,3,16,1152]{3,2,1,0:T(8,128)}, u32[]{:S(2)}, u32[]{:S(2)}) async-start(f32[32,3,16,1152]{3,2,1,0:T(8,128)} %pack.2), calls=%async_computation.2 | async-start | bytes 14155776 | tf_op jit(solution)/shard_map/all_to_all | solution.py:26
  137.6 8.6 %gram.2 = f32[576,576]{1,0:T(8,128)} custom-call(f32[1536,1152]{1,0:T(8,128)} %bitcast.3.in_ref), custom_call_target="tpu_custom_call" | custom-call | flops 3774873600 | bytes 8404992 | tf_op jit(solution)/shard_map/gram/pallas_call | solution.py:175
  146.3 74.6 %all-to-all-done.2 = f32[32,3,16,1152]{3,2,1,0:T(8,128)} async-done(((f32[32,3,16,1152]{3,2,1,0:T(8,128)}), f32[32,3,16,1152]{3,2,1,0:T(8,128)}, u32[]{:S(2)}, u32[]{:S(2)}) %all-to-all-start.2) | async-done | bytes 7077920 | tf_op jit(solution)/shard_map/all_to_all | solution.py:26
  220.8 8.6 %gram.3 = f32[576,576]{1,0:T(8,128)} custom-call(f32[1536,1152]{1,0:T(8,128)} %bitcast.4.in_ref), custom_call_target="tpu_custom_call" | custom-call | flops 3774873600 | bytes 8404992 | tf_op jit(solution)/shard_map/gram/pallas_call | solution.py:175
  229.5 17.8 %all_to_all.36.images_ref = f32[32,8,576]{2,1,0:T(8,128)} all-to-all(f32[32,8,576]{2,1,0:T(8,128)S(1)} %broadcast_in_dim.2), channel_id=1, replica_groups=mesh['row'=8,'col'=8,'track'=4] {'row','track'}, dimensions={0} | all-to-all | bytes 1179648 | tf_op jit(solution)/shard_map/all_to_all | solution.py:26
  247.3 5.2 %iterate.1 = (f32[32,2,576]{2,1,0:T(2,128)}, f32[5,8,576]{2,1,0:T(8,128)}) custom-call(s32[2,64]{1,0:T(2,128)} %bitcast.20, f32[64,2,16,576]{3,2,1,0:T(8,128)} %factors_ref.9, f32[5,8,576]{2,1,0:T(8,128)} %get-tuple-element.25.state_ref, f32[32,8,576]{2,1,0:T(8,128)} %all_to_all.36.images_ref), custom_call_target="tpu_custom_call" | custom-call | tf_op jit(solution)/shard_map/iterate/pallas_call | solution.py:385
  252.5 13.0 %all_to_all.37.in_ref = f32[32,2,576]{2,1,0:T(2,128)} all-to-all(f32[32,2,576]{2,1,0:T(2,128)} %get-tuple-element.32), channel_id=1, replica_groups=mesh['row'=8,'col'=8,'track'=4] {'row','track'}, dimensions={0} | all-to-all | bytes 294912 | tf_op jit(solution)/shard_map/all_to_all | solution.py:26
  267.0 7.8 %all-to-all-start.6 = ((f32[8,2,576]{2,1,0:T(2,128)}), f32[8,2,576]{2,1,0:T(2,128)S(1)}, u32[]{:S(2)}, u32[]{:S(2)}) async-start(f32[8,2,576]{2,1,0:T(2,128)} %relay.3), calls=%async_computation.6 | async-start | bytes 81920 | tf_op jit(solution)/shard_map/all_to_all | solution.py:26
  274.8 4.0 %collective-permute-start.7 = (f32[72,576]{1,0:T(8,128)}, f32[72,576]{1,0:T(8,128)S(1)}, u32[]{:S(2)}, u32[]{:S(2)}) collective-permute-start(f32[72,576]{1,0:T(8,128)} %reduce-scatter.9.cloned.1.call-done), channel_id=1, source_target_pairs={{4,0},{5,8},{6,16},{7,24},{12,1},{13,9},{14,17},{15,25},{20,2},{21... | collective-permute-start | bytes 497672 | tf_op jit(solution)/shard_map/ppermute | solution.py:206
  280.6 3.0 collective-permute-start.9
  286.6 10.0 %collective-permute-done.7 = f32[72,576]{1,0:T(8,128)S(1)} collective-permute-done((f32[72,576]{1,0:T(8,128)}, f32[72,576]{1,0:T(8,128)S(1)}, u32[]{:S(2)}, u32[]{:S(2)}) %collective-permute-start.7) | collective-permute-done | bytes 165920 | tf_op jit(solution)/shard_map/ppermute | solution.py:206
  296.6 8.2 %collective-permute-done.9 = f32[72,576]{1,0:T(8,128)S(1)} collective-permute-done((f32[72,576]{1,0:T(8,128)}, f32[72,576]{1,0:T(8,128)S(1)}, u32[]{:S(2)}, u32[]{:S(2)}) %collective-permute-start.9) | collective-permute-done | bytes 165920 | tf_op jit(solution)/shard_map/ppermute | solution.py:206
  (38 shorter events, 24.4 us)
Async XLA Ops:
  25.5 13.6 %all-to-all-start.1 = ((f32[4,8,576]{2,1,0:T(8,128)}), f32[4,8,576]{2,1,0:T(8,128)S(1)}, u32[]{:S(2)}, u32[]{:S(2)}) async-start(f32[4,8,576]{2,1,0:T(8,128)} %get-tuple-element.21), calls=%async_computation.1 | async-start | bytes 163840 | tf_op jit(solution)/shard_map/all_to_all | solution.py:26
  39.1 0.6 copy-start
  41.2 6.6 %copy-start.2 = (f32[1,8,576]{2,1,0:T(8,128)S(1)}, f32[1,8,576]{2,1,0:T(8,128)}, u32[]{:S(2)}) copy-start(f32[1,8,576]{2,1,0:T(8,128)} %relay.2) | copy-start | bytes 55300
  41.2 89.9 %all-to-all-start.3 = ((f32[32,3,16,1152]{3,2,1,0:T(8,128)}), f32[32,3,16,1152]{3,2,1,0:T(8,128)}, u32[]{:S(2)}, u32[]{:S(2)}) async-start(f32[32,3,16,1152]{3,2,1,0:T(8,128)} %pack.3), calls=%async_computation.3 | async-start | bytes 14155776 | tf_op jit(solution)/shard_map/all_to_all | solution.py:26
  47.8 3.1 collective-permute-start
  51.0 4.7 %collective-permute-start.1 = (f32[8,576]{1,0:T(8,128)S(1)}, f32[8,576]{1,0:T(8,128)S(1)}, u32[]{:S(2)}, u32[]{:S(2)}) collective-permute-start(f32[8,576]{1,0:T(8,128)S(1)} %add.32), channel_id=1, source_target_pairs={{0,8},{4,12},{8,0},{12,4},{16,24},{20,28},{24,16},{28,20},{1,9},{5... | collective-permute-start | bytes 55304 | tf_op jit(solution)/shard_map/ppermute | solution.py:53
  55.7 6.6 %collective-permute-start.2 = (f32[8,576]{1,0:T(8,128)S(1)}, f32[8,576]{1,0:T(8,128)S(1)}, u32[]{:S(2)}, u32[]{:S(2)}) collective-permute-start(f32[8,576]{1,0:T(8,128)S(1)} %add.33), channel_id=1, source_target_pairs={{0,16},{4,20},{8,24},{12,28},{16,0},{20,4},{24,8},{28,12},{1,17},{... | collective-permute-start | bytes 55304 | tf_op jit(solution)/shard_map/ppermute | solution.py:53
  67.5 3.2 %collective-permute-start.3 = (f32[8,576]{1,0:T(8,128)}, f32[8,576]{1,0:T(8,128)S(1)}, u32[]{:S(2)}, u32[]{:S(2)}) collective-permute-start(f32[8,576]{1,0:T(8,128)} %get-tuple-element.23), channel_id=1, source_target_pairs={{0,4},{4,0},{8,12},{12,8},{16,20},{20,16},{24,28},{28,24},{1,5},{5... | collective-permute-start | bytes 55304 | tf_op jit(solution)/shard_map/ppermute | solution.py:53
  71.4 3.9 %collective-permute-start.4 = (f32[8,576]{1,0:T(8,128)S(1)}, f32[8,576]{1,0:T(8,128)S(1)}, u32[]{:S(2)}, u32[]{:S(2)}) collective-permute-start(f32[8,576]{1,0:T(8,128)S(1)} %add.35), channel_id=1, source_target_pairs={{0,8},{4,12},{8,0},{12,4},{16,24},{20,28},{24,16},{28,20},{1,9},{5... | collective-permute-start | bytes 55304 | tf_op jit(solution)/shard_map/ppermute | solution.py:53
  75.4 14.3 %collective-permute-start.5 = (f32[8,576]{1,0:T(8,128)S(1)}, f32[8,576]{1,0:T(8,128)S(1)}, u32[]{:S(2)}, u32[]{:S(2)}) collective-permute-start(f32[8,576]{1,0:T(8,128)S(1)} %add.36), channel_id=1, source_target_pairs={{0,16},{4,20},{8,24},{12,28},{16,0},{20,4},{24,8},{28,12},{1,17},{... | collective-permute-start | bytes 55304 | tf_op jit(solution)/shard_map/ppermute | solution.py:53
  131.1 89.7 %all-to-all-start.2 = ((f32[32,3,16,1152]{3,2,1,0:T(8,128)}), f32[32,3,16,1152]{3,2,1,0:T(8,128)}, u32[]{:S(2)}, u32[]{:S(2)}) async-start(f32[32,3,16,1152]{3,2,1,0:T(8,128)} %pack.2), calls=%async_computation.2 | async-start | bytes 14155776 | tf_op jit(solution)/shard_map/all_to_all | solution.py:26
  137.6 137.3 %reduce-scatter.9.cloned.1.call-start = ((), (), s32[]{:S(2)}) async-start(), calls=%async_computation.10 | async-start | bytes 1658880
  146.2 134.4 %reduce-scatter.7.cloned.1.call-start = ((), (), s32[]{:S(2)}) async-start(), calls=%async_computation.9 | async-start | bytes 1658880
  267.0 13.6 %all-to-all-start.6 = ((f32[8,2,576]{2,1,0:T(2,128)}), f32[8,2,576]{2,1,0:T(2,128)S(1)}, u32[]{:S(2)}, u32[]{:S(2)}) async-start(f32[8,2,576]{2,1,0:T(2,128)} %relay.3), calls=%async_computation.6 | async-start | bytes 81920 | tf_op jit(solution)/shard_map/all_to_all | solution.py:26
  274.8 21.8 %collective-permute-start.7 = (f32[72,576]{1,0:T(8,128)}, f32[72,576]{1,0:T(8,128)S(1)}, u32[]{:S(2)}, u32[]{:S(2)}) collective-permute-start(f32[72,576]{1,0:T(8,128)} %reduce-scatter.9.cloned.1.call-done), channel_id=1, source_target_pairs={{4,0},{5,8},{6,16},{7,24},{12,1},{13,9},{14,17},{15,25},{20,2},{21... | collective-permute-start | bytes 497672 | tf_op jit(solution)/shard_map/ppermute | solution.py:206
  278.8 17.8 %collective-permute-start.6 = (f32[72,576]{1,0:T(8,128)}, f32[72,576]{1,0:T(8,128)S(1)}, u32[]{:S(2)}, u32[]{:S(2)}) collective-permute-start(f32[72,576]{1,0:T(8,128)} %reduce-scatter.9.cloned.1.call-done), channel_id=1, source_target_pairs={{0,0},{1,8},{2,16},{3,24},{8,1},{9,9},{10,17},{11,25},{16,2},{17,1... | collective-permute-start | bytes 497672 | tf_op jit(solution)/shard_map/ppermute | solution.py:206
  280.6 4.3 %copy-start.1 = (f32[8,2,576]{2,1,0:T(2,128)}, f32[8,2,576]{2,1,0:T(2,128)S(1)}, u32[]{:S(2)}) copy-start(f32[8,2,576]{2,1,0:T(2,128)S(1)} %all-to-all-done.6.images_ref) | copy-start | bytes 110596
  280.6 24.2 %collective-permute-start.9 = (f32[72,576]{1,0:T(8,128)}, f32[72,576]{1,0:T(8,128)S(1)}, u32[]{:S(2)}, u32[]{:S(2)}) collective-permute-start(f32[72,576]{1,0:T(8,128)} %reduce-scatter.7.cloned.1.call-done), channel_id=1, source_target_pairs={{4,4},{5,12},{6,20},{7,28},{12,5},{13,13},{14,21},{15,29},{20,6},{... | collective-permute-start | bytes 497672 | tf_op jit(solution)/shard_map/ppermute | solution.py:206
  283.7 23.2 %collective-permute-start.8 = (f32[72,576]{1,0:T(8,128)}, f32[72,576]{1,0:T(8,128)S(1)}, u32[]{:S(2)}, u32[]{:S(2)}) collective-permute-start(f32[72,576]{1,0:T(8,128)} %reduce-scatter.7.cloned.1.call-done), channel_id=1, source_target_pairs={{0,4},{1,12},{2,20},{3,28},{8,5},{9,13},{10,21},{11,29},{16,6},{17... | collective-permute-start | bytes 497672 | tf_op jit(solution)/shard_map/ppermute | solution.py:206
Sparse Core Ops, SparseCore 0:
  146.3 37.4 reduce-scatter.8
  229.6 36.3 reduce-scatter.6

commit v2 on v1

--- a/solution.py
+++ b/solution.py
@@ -390,7 +390,9 @@
         scratch_shapes=[spread, spread],
         name="iterate",
     )(track_clusters, factors, state, exchange(part, ("row", "track")))
-    part = exchange(relay(exchange(part, ("row", "track")), n_col), "col")
+    part = relay(exchange(part, ("row", "track")), n_col)
+    part, even_out = lax.optimization_barrier((part, even_out))
+    part = exchange(part, "col")
     piece, part = lax.optimization_barrier((piece, part))
     odd_out = placed(piece, 1)
     row_id = lax.axis_index("row").astype(jnp.int32).reshape(1)

time: 316 us -> 327 us (1.035)
  starting transfers between devices: 51 us -> 71.6 us
  blocking collectives: 43.5 us -> 25.7 us
  waiting for transfers between devices: 148 us -> 155 us
    all_to_all x4 -> x5, starting transfers between devices: 25.2 us -> 46.2 us  [exchange(): return lax.all_to_all(copies, axis, 0, 0, tiled=True)]
    all_to_all x3 -> x2, blocking collectives: 43.5 us -> 25.7 us  [exchange(): return lax.all_to_all(copies, axis, 0, 0, tiled=True)]
    all_to_all x4 -> x5, waiting for transfers between devices: 117 us -> 129 us  [exchange(): return lax.all_to_all(copies, axis, 0, 0, tiled=True)]
    ppermute x4, waiting for transfers between devices: 20.2 us -> 16.3 us  [placed(): out.append(lax.ppermute(piece, ('col', 'track'), moves))]
  transfers between devices with their start and end apart: 16 -> 17, of which waited for: 11 -> 11; matrix products, arithmetic and copies ran while one was open for 0% -> 1% of each run, Pallas kernels for 15% -> 15%
where the time goes in v2:
time: 327 us; the launch traced here: 326 us
  waiting for transfers between devices  155 us (47%)
  starting transfers between devices  71.6 us (22%)
  Pallas kernels  55.2 us (17%)
  blocking collectives  25.7 us (8%)
  between operations  14.2 us (4%)
    all_to_all x5, waiting for transfers between devices, exchange(): return lax.all_to_all(copies, axis, 0, 0, tiled=True)  129 us
    all_to_all x5, starting transfers between devices, exchange(): return lax.all_to_all(copies, axis, 0, 0, tiled=True)  46.2 us
    all_to_all x2, blocking collectives, exchange(): return lax.all_to_all(copies, axis, 0, 0, tiled=True)  25.7 us
    pallas_call x2, Pallas kernels, pack(): pl.pallas_call(functools.partial(pack_kernel, parity, tracks), grid=(PACK...  18 us
    pallas_call x2, Pallas kernels, gram(): pl.pallas_call(functools.partial(gram_kernel, params), grid=(GRAM_STEPS,)...  17.2 us
    ppermute x6, starting transfers between devices, sum_over_planes(): value = value + lax.ppermute(value, 'col', pairs)  16.9 us
    ppermute x4, waiting for transfers between devices, placed(): out.append(lax.ppermute(piece, ('col', 'track'), moves))  16.3 us
    ppermute x6, waiting for transfers between devices, sum_over_planes(): value = value + lax.ppermute(value, 'col', pairs)  9.89 us
  transfers between devices with their start and end apart: 17, of which 11 were waited for; matrix products, arithmetic and copies ran while one was open for 1% of the time, Pallas kernels for 15%

profile of v2, /device:TPU:35, one launch (start us, length us, event | category | flops | bytes accessed | tf_op | source)
XLA Modules:
  0.0 326.0 jit_solution(15744801449826625681)
XLA Ops:
  7.2 4.0 %diag.1 = f32[8,16,576]{2,1,0:T(8,128)} custom-call(s32[2,64]{1,0:T(2,128)} %bitcast.10, f32[64,2,16,576]{3,2,1,0:T(8,128)} %factors_ref.9, f32[1,576]{1,0:T(1,128)} %damping_ref.1, f32[1,576]{1,0:T(1,128)} %rhs_ref.1), custom_call_target="tpu_custom_call" | custom-call | tf_op jit(solution)/shard_map/diag/pallas_call | solution.py:347
  11.2 12.7 %all_to_all.35.in_ref = f32[8,16,576]{2,1,0:T(8,128)} all-to-all(f32[8,16,576]{2,1,0:T(8,128)} %diag.1), channel_id=1, replica_groups=mesh['row'=8,'col'=8,'track'=4] {'row'}, dimensions={0} | all-to-all | bytes 589824 | tf_op jit(solution)/shard_map/all_to_all | solution.py:26
  25.5 4.3 %all-to-all-start.1 = ((f32[4,8,576]{2,1,0:T(8,128)}), f32[4,8,576]{2,1,0:T(8,128)S(1)}, u32[]{:S(2)}, u32[]{:S(2)}) async-start(f32[4,8,576]{2,1,0:T(8,128)} %get-tuple-element.23), calls=%async_computation.1 | async-start | bytes 163840 | tf_op jit(solution)/shard_map/all_to_all | solution.py:26
  29.8 9.2 %pack.3 = f32[32,3,16,1152]{3,2,1,0:T(8,128)} custom-call(s32[2,64]{1,0:T(2,128)} %bitcast.11, s32[64]{0:T(128)} %flip_ref.3, f32[64,2,16,576]{3,2,1,0:T(8,128)} %factors_ref.9), custom_call_target="tpu_custom_call" | custom-call | bytes 11796480 | tf_op jit(solution)/shard_map/pack/pallas_call | solution.py:115
  41.1 6.6 %all-to-all-start.3 = ((f32[32,3,16,1152]{3,2,1,0:T(8,128)}), f32[32,3,16,1152]{3,2,1,0:T(8,128)}, u32[]{:S(2)}, u32[]{:S(2)}) async-start(f32[32,3,16,1152]{3,2,1,0:T(8,128)} %pack.3), calls=%async_computation.3 | async-start | bytes 14155776 | tf_op jit(solution)/shard_map/all_to_all | solution.py:26
  50.8 3.0 collective-permute-start.1
  55.4 5.3 %collective-permute-start.2 = (f32[8,576]{1,0:T(8,128)S(1)}, f32[8,576]{1,0:T(8,128)S(1)}, u32[]{:S(2)}, u32[]{:S(2)}) collective-permute-start(f32[8,576]{1,0:T(8,128)S(1)} %add.26), channel_id=1, source_target_pairs={{0,16},{4,20},{8,24},{12,28},{16,0},{20,4},{24,8},{28,12},{1,17},{... | collective-permute-start | bytes 55304 | tf_op jit(solution)/shard_map/ppermute | solution.py:53
  62.6 4.5 %begin.1 = (f32[8,576]{1,0:T(8,128)}, f32[5,8,576]{2,1,0:T(8,128)}) custom-call(s32[2,64]{1,0:T(2,128)} %bitcast.12, f32[64,2,16,576]{3,2,1,0:T(8,128)} %factors_ref.9, f32[2,8,576]{2,1,0:T(8,128)} %get-tuple-element.22.vectors_ref, f32[8,576]{1,0:T(8,128)} %add.27.diag_ref), custom_call_target="tpu_custom_call" | custom-call | tf_op jit(solution)/shard_map/begin/pallas_call | solution.py:367
  75.1 5.2 %collective-permute-start.5 = (f32[8,576]{1,0:T(8,128)S(1)}, f32[8,576]{1,0:T(8,128)S(1)}, u32[]{:S(2)}, u32[]{:S(2)}) collective-permute-start(f32[8,576]{1,0:T(8,128)S(1)} %add.29), channel_id=1, source_target_pairs={{0,16},{4,20},{8,24},{12,28},{16,0},{20,4},{24,8},{28,12},{1,17},{... | collective-permute-start | bytes 55304 | tf_op jit(solution)/shard_map/ppermute | solution.py:53
  80.4 8.8 %pack.2 = f32[32,3,16,1152]{3,2,1,0:T(8,128)} custom-call(s32[2,64]{1,0:T(2,128)} %bitcast.13, s32[64]{0:T(128)} %flip_ref.3, f32[64,2,16,576]{3,2,1,0:T(8,128)} %factors_ref.9), custom_call_target="tpu_custom_call" | custom-call | bytes 11796480 | tf_op jit(solution)/shard_map/pack/pallas_call | solution.py:115
  90.1 40.9 %all-to-all-done.3 = f32[32,3,16,1152]{3,2,1,0:T(8,128)} async-done(((f32[32,3,16,1152]{3,2,1,0:T(8,128)}), f32[32,3,16,1152]{3,2,1,0:T(8,128)}, u32[]{:S(2)}, u32[]{:S(2)}) %all-to-all-start.3) | async-done | bytes 7077920 | tf_op jit(solution)/shard_map/all_to_all | solution.py:26
  131.0 6.5 %all-to-all-start.2 = ((f32[32,3,16,1152]{3,2,1,0:T(8,128)}), f32[32,3,16,1152]{3,2,1,0:T(8,128)}, u32[]{:S(2)}, u32[]{:S(2)}) async-start(f32[32,3,16,1152]{3,2,1,0:T(8,128)} %pack.2), calls=%async_computation.2 | async-start | bytes 14155776 | tf_op jit(solution)/shard_map/all_to_all | solution.py:26
  137.5 8.6 %gram.2 = f32[576,576]{1,0:T(8,128)} custom-call(f32[1536,1152]{1,0:T(8,128)} %bitcast.3.in_ref), custom_call_target="tpu_custom_call" | custom-call | flops 3774873600 | bytes 8404992 | tf_op jit(solution)/shard_map/gram/pallas_call | solution.py:175
  146.2 74.5 %all-to-all-done.2 = f32[32,3,16,1152]{3,2,1,0:T(8,128)} async-done(((f32[32,3,16,1152]{3,2,1,0:T(8,128)}), f32[32,3,16,1152]{3,2,1,0:T(8,128)}, u32[]{:S(2)}, u32[]{:S(2)}) %all-to-all-start.2) | async-done | bytes 7077920 | tf_op jit(solution)/shard_map/all_to_all | solution.py:26
  220.7 8.6 %gram.3 = f32[576,576]{1,0:T(8,128)} custom-call(f32[1536,1152]{1,0:T(8,128)} %bitcast.4.in_ref), custom_call_target="tpu_custom_call" | custom-call | flops 3774873600 | bytes 8404992 | tf_op jit(solution)/shard_map/gram/pallas_call | solution.py:175
  229.3 6.4 %all-to-all-start.4 = ((f32[32,8,576]{2,1,0:T(8,128)}), f32[32,8,576]{2,1,0:T(8,128)S(1)}, u32[]{:S(2)}, u32[]{:S(2)}) async-start(f32[32,8,576]{2,1,0:T(8,128)} %broadcast_in_dim.4), calls=%async_computation.4 | async-start | bytes 1310720 | tf_op jit(solution)/shard_map/all_to_all | solution.py:26
  235.8 3.4 %collective-permute-start.7 = (f32[72,576]{1,0:T(8,128)}, f32[72,576]{1,0:T(8,128)S(1)}, u32[]{:S(2)}, u32[]{:S(2)}) collective-permute-start(f32[72,576]{1,0:T(8,128)} %reduce-scatter.9.cloned.1.call-done), channel_id=1, source_target_pairs={{4,0},{5,8},{6,16},{7,24},{12,1},{13,9},{14,17},{15,25},{20,2},{21... | collective-permute-start | bytes 497672 | tf_op jit(solution)/shard_map/ppermute | solution.py:206
  239.9 7.4 %all-to-all-done.4.images_ref = f32[32,8,576]{2,1,0:T(8,128)S(1)} async-done(((f32[32,8,576]{2,1,0:T(8,128)}), f32[32,8,576]{2,1,0:T(8,128)S(1)}, u32[]{:S(2)}, u32[]{:S(2)}) %all-to-all-start.4) | async-done | bytes 589856 | tf_op jit(solution)/shard_map/all_to_all | solution.py:26
  248.1 5.2 %iterate.1 = (f32[32,2,576]{2,1,0:T(2,128)}, f32[5,8,576]{2,1,0:T(8,128)}) custom-call(s32[2,64]{1,0:T(2,128)} %bitcast.14, f32[64,2,16,576]{3,2,1,0:T(8,128)} %factors_ref.9, f32[5,8,576]{2,1,0:T(8,128)} %get-tuple-element.27.state_ref, f32[32,8,576]{2,1,0:T(8,128)} %copy-done), custom_call_target="tpu_custom_call" | custom-call | tf_op jit(solution)/shard_map/iterate/pallas_call | solution.py:385
  253.3 13.0 %all_to_all.36.in_ref = f32[32,2,576]{2,1,0:T(2,128)} all-to-all(f32[32,2,576]{2,1,0:T(2,128)} %get-tuple-element.34), channel_id=1, replica_groups=mesh['row'=8,'col'=8,'track'=4] {'row','track'}, dimensions={0} | all-to-all | bytes 294912 | tf_op jit(solution)/shard_map/all_to_all | solution.py:26
  267.9 22.4 %all-to-all-start.6 = ((f32[8,2,576]{2,1,0:T(2,128)}), f32[8,2,576]{2,1,0:T(2,128)S(1)}, u32[]{:S(2)}, u32[]{:S(2)}) async-start(f32[8,2,576]{2,1,0:T(2,128)} %relay.3), calls=%async_computation.6 | async-start | bytes 81920 | tf_op jit(solution)/shard_map/all_to_all | solution.py:26
  290.3 5.8 %all-to-all-done.6.images_ref = f32[8,2,576]{2,1,0:T(2,128)S(1)} async-done(((f32[8,2,576]{2,1,0:T(2,128)}), f32[8,2,576]{2,1,0:T(2,128)S(1)}, u32[]{:S(2)}, u32[]{:S(2)}) %all-to-all-start.6) | async-done | bytes 36896 | tf_op jit(solution)/shard_map/all_to_all | solution.py:26
  296.1 3.0 collective-permute-start.9
  304.4 14.0 %collective-permute-done.8 = f32[72,576]{1,0:T(8,128)S(1)} collective-permute-done((f32[72,576]{1,0:T(8,128)}, f32[72,576]{1,0:T(8,128)S(1)}, u32[]{:S(2)}, u32[]{:S(2)}) %collective-permute-start.8) | collective-permute-done | bytes 165920 | tf_op jit(solution)/shard_map/ppermute | solution.py:206
  (42 shorter events, 28.4 us)
Async XLA Ops:
  25.5 13.4 %all-to-all-start.1 = ((f32[4,8,576]{2,1,0:T(8,128)}), f32[4,8,576]{2,1,0:T(8,128)S(1)}, u32[]{:S(2)}, u32[]{:S(2)}) async-start(f32[4,8,576]{2,1,0:T(8,128)} %get-tuple-element.23), calls=%async_computation.1 | async-start | bytes 163840 | tf_op jit(solution)/shard_map/all_to_all | solution.py:26
  38.9 0.6 copy-start.1
  41.1 6.6 %copy-start.3 = (f32[1,8,576]{2,1,0:T(8,128)S(1)}, f32[1,8,576]{2,1,0:T(8,128)}, u32[]{:S(2)}) copy-start(f32[1,8,576]{2,1,0:T(8,128)} %relay.2) | copy-start | bytes 55300
  41.1 89.9 %all-to-all-start.3 = ((f32[32,3,16,1152]{3,2,1,0:T(8,128)}), f32[32,3,16,1152]{3,2,1,0:T(8,128)}, u32[]{:S(2)}, u32[]{:S(2)}) async-start(f32[32,3,16,1152]{3,2,1,0:T(8,128)} %pack.3), calls=%async_computation.3 | async-start | bytes 14155776 | tf_op jit(solution)/shard_map/all_to_all | solution.py:26
  47.7 3.1 collective-permute-start
  50.8 4.6 %collective-permute-start.1 = (f32[8,576]{1,0:T(8,128)S(1)}, f32[8,576]{1,0:T(8,128)S(1)}, u32[]{:S(2)}, u32[]{:S(2)}) collective-permute-start(f32[8,576]{1,0:T(8,128)S(1)} %add.25), channel_id=1, source_target_pairs={{0,8},{4,12},{8,0},{12,4},{16,24},{20,28},{24,16},{28,20},{1,9},{5... | collective-permute-start | bytes 55304 | tf_op jit(solution)/shard_map/ppermute | solution.py:53
  55.4 6.5 %collective-permute-start.2 = (f32[8,576]{1,0:T(8,128)S(1)}, f32[8,576]{1,0:T(8,128)S(1)}, u32[]{:S(2)}, u32[]{:S(2)}) collective-permute-start(f32[8,576]{1,0:T(8,128)S(1)} %add.26), channel_id=1, source_target_pairs={{0,16},{4,20},{8,24},{12,28},{16,0},{20,4},{24,8},{28,12},{1,17},{... | collective-permute-start | bytes 55304 | tf_op jit(solution)/shard_map/ppermute | solution.py:53
  67.1 3.2 collective-permute-start.3
  71.1 4.0 %collective-permute-start.4 = (f32[8,576]{1,0:T(8,128)S(1)}, f32[8,576]{1,0:T(8,128)S(1)}, u32[]{:S(2)}, u32[]{:S(2)}) collective-permute-start(f32[8,576]{1,0:T(8,128)S(1)} %add.28), channel_id=1, source_target_pairs={{0,8},{4,12},{8,0},{12,4},{16,24},{20,28},{24,16},{28,20},{1,9},{5... | collective-permute-start | bytes 55304 | tf_op jit(solution)/shard_map/ppermute | solution.py:53
  75.1 14.1 %collective-permute-start.5 = (f32[8,576]{1,0:T(8,128)S(1)}, f32[8,576]{1,0:T(8,128)S(1)}, u32[]{:S(2)}, u32[]{:S(2)}) collective-permute-start(f32[8,576]{1,0:T(8,128)S(1)} %add.29), channel_id=1, source_target_pairs={{0,16},{4,20},{8,24},{12,28},{16,0},{20,4},{24,8},{28,12},{1,17},{... | collective-permute-start | bytes 55304 | tf_op jit(solution)/shard_map/ppermute | solution.py:53
  131.0 89.7 %all-to-all-start.2 = ((f32[32,3,16,1152]{3,2,1,0:T(8,128)}), f32[32,3,16,1152]{3,2,1,0:T(8,128)}, u32[]{:S(2)}, u32[]{:S(2)}) async-start(f32[32,3,16,1152]{3,2,1,0:T(8,128)} %pack.2), calls=%async_computation.2 | async-start | bytes 14155776 | tf_op jit(solution)/shard_map/all_to_all | solution.py:26
  137.4 98.3 %reduce-scatter.9.cloned.1.call-start = ((), (), s32[]{:S(2)}) async-start(), calls=%async_computation.10 | async-start | bytes 1658880
  146.1 144.2 %reduce-scatter.7.cloned.1.call-start = ((), (), s32[]{:S(2)}) async-start(), calls=%async_computation.9 | async-start | bytes 1658880
  229.3 18.0 %all-to-all-start.4 = ((f32[32,8,576]{2,1,0:T(8,128)}), f32[32,8,576]{2,1,0:T(8,128)S(1)}, u32[]{:S(2)}, u32[]{:S(2)}) async-start(f32[32,8,576]{2,1,0:T(8,128)} %broadcast_in_dim.4), calls=%async_computation.4 | async-start | bytes 1310720 | tf_op jit(solution)/shard_map/all_to_all | solution.py:26
  235.8 32.1 %collective-permute-start.7 = (f32[72,576]{1,0:T(8,128)}, f32[72,576]{1,0:T(8,128)S(1)}, u32[]{:S(2)}, u32[]{:S(2)}) collective-permute-start(f32[72,576]{1,0:T(8,128)} %reduce-scatter.9.cloned.1.call-done), channel_id=1, source_target_pairs={{4,0},{5,8},{6,16},{7,24},{12,1},{13,9},{14,17},{15,25},{20,2},{21... | collective-permute-start | bytes 497672 | tf_op jit(solution)/shard_map/ppermute | solution.py:206
  239.2 28.6 %collective-permute-start.6 = (f32[72,576]{1,0:T(8,128)}, f32[72,576]{1,0:T(8,128)S(1)}, u32[]{:S(2)}, u32[]{:S(2)}) collective-permute-start(f32[72,576]{1,0:T(8,128)} %reduce-scatter.9.cloned.1.call-done), channel_id=1, source_target_pairs={{0,0},{1,8},{2,16},{3,24},{8,1},{9,9},{10,17},{11,25},{16,2},{17,1... | collective-permute-start | bytes 497672 | tf_op jit(solution)/shard_map/ppermute | solution.py:206
  247.3 0.8 copy-start
  267.9 28.2 %all-to-all-start.6 = ((f32[8,2,576]{2,1,0:T(2,128)}), f32[8,2,576]{2,1,0:T(2,128)S(1)}, u32[]{:S(2)}, u32[]{:S(2)}) async-start(f32[8,2,576]{2,1,0:T(2,128)} %relay.3), calls=%async_computation.6 | async-start | bytes 81920 | tf_op jit(solution)/shard_map/all_to_all | solution.py:26
  296.1 4.3 %copy-start.2 = (f32[8,2,576]{2,1,0:T(2,128)}, f32[8,2,576]{2,1,0:T(2,128)S(1)}, u32[]{:S(2)}) copy-start(f32[8,2,576]{2,1,0:T(2,128)S(1)} %all-to-all-done.6.images_ref) | copy-start | bytes 110596
  296.1 8.3 %collective-permute-start.9 = (f32[72,576]{1,0:T(8,128)}, f32[72,576]{1,0:T(8,128)S(1)}, u32[]{:S(2)}, u32[]{:S(2)}) collective-permute-start(f32[72,576]{1,0:T(8,128)} %reduce-scatter.7.cloned.1.call-done), channel_id=1, source_target_pairs={{4,4},{5,12},{6,20},{7,28},{12,5},{13,13},{14,21},{15,29},{20,6},{... | collective-permute-start | bytes 497672 | tf_op jit(solution)/shard_map/ppermute | solution.py:206
  299.1 19.3 %collective-permute-start.8 = (f32[72,576]{1,0:T(8,128)}, f32[72,576]{1,0:T(8,128)S(1)}, u32[]{:S(2)}, u32[]{:S(2)}) collective-permute-start(f32[72,576]{1,0:T(8,128)} %reduce-scatter.7.cloned.1.call-done), channel_id=1, source_target_pairs={{0,4},{1,12},{2,20},{3,28},{8,5},{9,13},{10,21},{11,29},{16,6},{17... | collective-permute-start | bytes 497672 | tf_op jit(solution)/shard_map/ppermute | solution.py:206
Sparse Core Ops, SparseCore 0:
  146.2 37.6 reduce-scatter.8
  229.4 46.9 reduce-scatter.6

commit v3 on v1

--- a/solution.py
+++ b/solution.py
@@ -10,7 +10,8 @@
 CAPACITY = 3
 LANES = 128
 PACK_STEPS = 8
-GRAM_STEPS = 3
+EARLY = ((0, 0), (0, 1), (0, 2), (1, 0), (1, 1))
+LATE = ((1, 2),)
 
 VMEM = pl.BlockSpec(memory_space=pltpu.VMEM)
 SMEM = pl.BlockSpec(memory_space=pltpu.SMEM)
@@ -55,7 +56,7 @@
     return value
 
 
-def pack_kernel(parity, tracks, clusters_ref, flip_ref, factors_ref, out_ref, counts, slots):
+def pack_kernel(chosen, tracks, clusters_ref, flip_ref, factors_ref, out_ref, counts, slots):
     step = pl.program_id(0)
     blocks, _, jac_rows, params = factors_ref.shape
     per_step = out_ref.shape[0]
@@ -88,7 +89,7 @@
         lax.fori_loop(0, blocks, assign, 0, unroll=4)
 
     for local in range(per_step):
-        for place in range(CAPACITY):
+        for at, (parity, place) in enumerate(chosen):
             pair = (step * per_step + local) * 2 + parity
             block = slots[pair * CAPACITY + place]
 
@@ -97,23 +98,23 @@
                 flip = flip_ref[block]
                 first = factors_ref[block, flip]
                 second = factors_ref[block, 1 - flip]
-                out_ref[local, place, :, 0:whole] = first[:, 0:whole]
-                out_ref[local, place, :, whole : whole + LANES] = jnp.concatenate(
+                out_ref[local, at, :, 0:whole] = first[:, 0:whole]
+                out_ref[local, at, :, whole : whole + LANES] = jnp.concatenate(
                     [first[:, whole:params], second[:, whole:params]], axis=1
                 )
-                out_ref[local, place, :, whole + LANES : 2 * params] = second[:, 0:whole]
+                out_ref[local, at, :, whole + LANES : 2 * params] = second[:, 0:whole]
 
             @pl.when(block < 0)
             def _():
-                out_ref[local, place] = jnp.zeros((jac_rows, 2 * params), jnp.float32)
-
-
-def pack(factors, track_clusters, filed_flip, parity, rows, tracks):
+                out_ref[local, at] = jnp.zeros((jac_rows, 2 * params), jnp.float32)
+
+
+def pack(factors, track_clusters, filed_flip, chosen, rows, tracks):
     jac_rows, params = factors.shape[2:]
-    shape = (rows * tracks, CAPACITY, jac_rows, 2 * params)
+    shape = (rows * tracks, len(chosen), jac_rows, 2 * params)
     pairs = 2 * rows * tracks
     return pl.pallas_call(
-        functools.partial(pack_kernel, parity, tracks),
+        functools.partial(pack_kernel, chosen, tracks),
         grid=(PACK_STEPS,),
         out_shape=jax.ShapeDtypeStruct(shape, jnp.float32),
         in_specs=[
@@ -130,18 +131,15 @@
         ],
         cost_estimate=pl.CostEstimate(
             flops=0,
-            bytes_accessed=4 * (factors.size + shape[0] * CAPACITY * jac_rows * 2 * params),
+            bytes_accessed=4 * (factors.size + shape[0] * shape[1] * jac_rows * 2 * params),
             transcendentals=0,
         ),
         name="pack",
     )(track_clusters, filed_flip, factors)
 
 
-def gram_kernel(params, in_ref, out_ref, total):
-    step = pl.program_id(0)
+def product_of(value, params):
     whole = params // LANES * LANES
-    wide = whole + LANES
-    value = in_ref[...]
     high = value.astype(jnp.bfloat16)
     low = (value - high.astype(jnp.float32)).astype(jnp.bfloat16)
     product = functools.partial(
@@ -149,62 +147,98 @@
         dimension_numbers=(((0,), (0,)), ((), ())),
         preferred_element_type=jnp.float32,
     )
-    first, second = slice(0, wide), slice(whole, 2 * params)
+    first, second = slice(0, whole + LANES), slice(whole, 2 * params)
     gram = product(high[:, first], high[:, second])
     gram = gram + product(high[:, first], low[:, second])
-    gram = gram + product(low[:, first], high[:, second])
-
-    @pl.when(step == 0)
-    def _():
-        total[...] = gram
-
-    @pl.when(step > 0)
-    def _():
-        total[...] += gram
+    return gram + product(low[:, first], high[:, second])
+
+
+def plane_of(parity, track, part, planes):
+    if parity == 0:
+        return (2 * track - part + planes) % planes
+    return (2 * track + 1 + part) % planes
+
+
+def store_parts(out_ref, total, parity, track, params, add=False):
+    planes, share = out_ref.shape[:2]
+    whole = params // LANES * LANES
+    wide = whole + LANES
+    for part in range(params // share):
+        plane = lax.rem(
+            2 * track - part + planes if parity == 0 else 2 * track + 1 + part, planes
+        )
+        rows = slice(part * share, (part + 1) * share)
+        main = total[rows, LANES:wide]
+        tail = total[rows, params - whole : LANES]
+        if add:
+            main = out_ref[plane, :, 0:whole] + main
+            tail = out_ref[plane, :, whole:params] + tail
+        out_ref[plane, :, 0:whole] = main
+        out_ref[plane, :, whole:params] = tail
+
+
+def early_kernel(params, track_ref, in_ref, out_ref, totals):
+    step = pl.program_id(0)
+    gram = product_of(in_ref[...].reshape(-1, 2 * params), params)
+    for at, (parity, place) in enumerate(EARLY):
+
+        @pl.when(step == at)
+        def _():
+            if place == 0:
+                totals[parity] = gram
+            else:
+                totals[parity] += gram
 
     @pl.when(step == pl.num_programs(0) - 1)
     def _():
-        out_ref[:, 0:whole] = total[0:params, LANES:wide]
-        out_ref[:, whole:params] = total[0:params, params - whole : LANES]
-
-
-def gram(received, params):
-    received = received.reshape(-1, 2 * params)
-    rows, width = received.shape
+        for parity in range(2):
+            store_parts(out_ref, totals.at[parity], parity, track_ref[0], params)
+
+
+def late_kernel(params, track_ref, in_ref, blocks_ref, out_ref, total):
+    out_ref[...] = blocks_ref[...]
+    total[...] = product_of(in_ref[...].reshape(-1, 2 * params), params)
+    store_parts(out_ref, total, 1, track_ref[0], params, add=True)
+
+
+def gram_cost(slots, params):
+    return pl.CostEstimate(
+        flops=6 * 512 * 640 * 640 * slots,
+        bytes_accessed=4 * (512 * 2 * params * slots + 2 * params * params),
+        transcendentals=0,
+    )
+
+
+def early_products(track, received, params, planes):
+    devices, slots, jac_rows, width = received.shape
+    share = 2 * params // planes
     wide = params // LANES * LANES + LANES
     return pl.pallas_call(
-        functools.partial(gram_kernel, params),
-        grid=(GRAM_STEPS,),
-        out_shape=jax.ShapeDtypeStruct((params, params), jnp.float32),
-        in_specs=[pl.BlockSpec((rows // GRAM_STEPS, width), lambda step: (step, 0))],
-        out_specs=pl.BlockSpec((params, params), lambda step: (0, 0)),
+        functools.partial(early_kernel, params),
+        grid=(slots,),
+        out_shape=jax.ShapeDtypeStruct((planes, share, params), jnp.float32),
+        in_specs=[
+            SMEM,
+            pl.BlockSpec((devices, 1, jac_rows, width), lambda step: (0, step, 0, 0)),
+        ],
+        out_specs=pl.BlockSpec((planes, share, params), lambda step: (0, 0, 0)),
+        scratch_shapes=[pltpu.VMEM((2, wide, wide), jnp.float32)],
+        cost_estimate=gram_cost(slots, params),
+        name="early",
+    )(track, received)
+
+
+def late_products(track, received, blocks, params):
+    wide = params // LANES * LANES + LANES
+    return pl.pallas_call(
+        functools.partial(late_kernel, params),
+        out_shape=jax.ShapeDtypeStruct(blocks.shape, jnp.float32),
+        in_specs=[SMEM, VMEM, VMEM],
+        out_specs=VMEM,
         scratch_shapes=[pltpu.VMEM((wide, wide), jnp.float32)],
-        cost_estimate=pl.CostEstimate(
-            flops=6 * rows * wide * wide,
-            bytes_accessed=4 * (rows * width + params * params),
-            transcendentals=0,
-        ),
-        name="gram",
-    )(received)
-
-
-def plane_rows(block):
-    return lax.psum_scatter(block, "col", scatter_dimension=0, tiled=True)
-
-
-def placed(piece, parity):
-    n_col = lax.axis_size("col")
-    n_track = lax.axis_size("track")
-    halves = n_col // n_track
-    out = []
-    for half in range(halves):
-        moves = []
-        for col in range(half, n_col, halves):
-            for track in range(n_track):
-                target = (2 * track + parity) * n_track + col // halves
-                moves.append((col * n_track + track, target))
-        out.append(lax.ppermute(piece, ("col", "track"), moves))
-    return jnp.concatenate(out, axis=0)
+        cost_estimate=gram_cost(received.shape[1], params),
+        name="late",
+    )(track, received, blocks)
 
 
 def diag_kernel(clusters_ref, factors_ref, damping_ref, rhs_ref, out_ref, sums):
@@ -352,7 +386,7 @@
         scratch_shapes=[spread],
         name="diag",
     )(track_clusters, factors, damping, rhs)
-    even = pack(factors, track_clusters, filed_flip, 0, n_row, n_track)
+    early = pack(factors, track_clusters, filed_flip, EARLY, n_row, n_track)
     squares, vectors = pl.pallas_call(
         settle_kernel,
         out_shape=(shape_of(n_track, clusters, params), shape_of(2, clusters, params)),
@@ -362,8 +396,8 @@
     )(exchange(squares, "row"))
     squares = relay(exchange(squares, "track"), 1)[0]
 
-    even, squares = lax.optimization_barrier((even, squares))
-    even = exchange(even, ("row", "track"))
+    early, squares = lax.optimization_barrier((early, squares))
+    early = exchange(early, ("row", "track"))
     part, state = pl.pallas_call(
         begin_kernel,
         out_shape=(shape_of(clusters, params), state_shape),
@@ -374,13 +408,14 @@
     )(track_clusters, factors, vectors, sum_over_planes(squares))
     part = sum_over_planes(part)
     part = jnp.broadcast_to(part[None], (n_row * n_track,) + part.shape)
-    odd = pack(factors, track_clusters, filed_flip, 1, n_row, n_track)
-    odd, part, state = lax.optimization_barrier((odd, part, state))
-    odd = exchange(odd, ("row", "track"))
-    block = gram(even, params)
-    even_out = placed(plane_rows(block), 0)
-    odd, part, block = lax.optimization_barrier((odd, part, block))
-    piece = plane_rows(gram(odd, params))
+    late = pack(factors, track_clusters, filed_flip, LATE, n_row, n_track)
+    late, part, state = lax.optimization_barrier((late, part, state))
+    late = exchange(late, ("row", "track"))
+    track = lax.axis_index("track").astype(jnp.int32).reshape(1)
+    blocks = early_products(track, early, params, n_col)
+    late, part, blocks = lax.optimization_barrier((late, part, blocks))
+    blocks = late_products(track, late, blocks, params).reshape(2 * params, params)
+    piece = lax.psum_scatter(blocks, "col", scatter_dimension=0, tiled=True)
 
     part, state = pl.pallas_call(
         iterate_kernel,
@@ -392,7 +427,16 @@
     )(track_clusters, factors, state, exchange(part, ("row", "track")))
     part = exchange(relay(exchange(part, ("row", "track")), n_col), "col")
     piece, part = lax.optimization_barrier((piece, part))
-    odd_out = placed(piece, 1)
+    moves = [
+        (
+            plane_of(parity, track, part_at, n_col) * n_track + track,
+            (2 * track + parity) * n_track + part_at,
+        )
+        for parity in range(2)
+        for track in range(n_track)
+        for part_at in range(n_track)
+    ]
+    blocks_out = lax.ppermute(piece, ("col", "track"), moves)[None, None]
     row_id = lax.axis_index("row").astype(jnp.int32).reshape(1)
     solution_out, scaled = pl.pallas_call(
         finish_kernel,
@@ -402,7 +446,7 @@
         scratch_shapes=[pltpu.VMEM((5, clusters, 1, params), jnp.float32)],
         name="finish",
     )(row_id, state, part)
-    return solution_out, scaled, (even_out + odd_out)[None, None]
+    return solution_out, scaled, blocks_out
 
 
 def solution(mesh):

time: 316 us -> 336 us (1.063)
  starting transfers between devices: 51 us -> 36.8 us
  waiting for transfers between devices: 148 us -> 162 us
  blocking collectives: 43.5 us -> 57 us
    all_to_all x3 -> x4, blocking collectives: 43.5 us -> 57 us  [exchange(): return lax.all_to_all(copies, axis, 0, 0, tiled=True)]
    all_to_all x4 -> x3, waiting for transfers between devices: 117 us -> 128 us  [exchange(): return lax.all_to_all(copies, axis, 0, 0, tiled=True)]
    all_to_all x4 -> x3, starting transfers between devices: 25.2 us -> 17.5 us  [exchange(): return lax.all_to_all(copies, axis, 0, 0, tiled=True)]
    ppermute x4 -> x1, starting transfers between devices: 8.96 us -> 2.02 us  [on_device(): blocks_out = lax.ppermute(piece, ('col', 'track'), moves)[None, None]]
    ppermute x4 -> x1, waiting for transfers between devices: 20.2 us -> 24.4 us  [on_device(): blocks_out = lax.ppermute(piece, ('col', 'track'), moves)[None, None]]
  transfers between devices with their start and end apart: 16 -> 11, of which waited for: 11 -> 8; matrix products, arithmetic and copies ran while one was open for 0% -> 0% of each run, Pallas kernels for 15% -> 13%
where the time goes in v3:
time: 336 us; the launch traced here: 332 us
  waiting for transfers between devices  162 us (48%)
  Pallas kernels  57.3 us (17%)
  blocking collectives  57 us (17%)
  starting transfers between devices  36.8 us (11%)
  between operations  14.1 us (4%)
    all_to_all x3, waiting for transfers between devices, exchange(): return lax.all_to_all(copies, axis, 0, 0, tiled=True)  128 us
    all_to_all x4, blocking collectives, exchange(): return lax.all_to_all(copies, axis, 0, 0, tiled=True)  57 us
    ppermute x1, waiting for transfers between devices, on_device(): blocks_out = lax.ppermute(piece, ('col', 'track'), moves)[None, None]  24.4 us
    pallas_call x2, Pallas kernels, pack(): pl.pallas_call(functools.partial(pack_kernel, chosen, tracks), grid=(PACK...  18.2 us
    all_to_all x3, starting transfers between devices, exchange(): return lax.all_to_all(copies, axis, 0, 0, tiled=True)  17.5 us
    ppermute x6, starting transfers between devices, sum_over_planes(): value = value + lax.ppermute(value, 'col', pairs)  17.1 us
    pallas_call x1, Pallas kernels, early_products(): pl.pallas_call(functools.partial(early_kernel, params), grid=(slots,), ou...  13.1 us
    ppermute x6, waiting for transfers between devices, sum_over_planes(): value = value + lax.ppermute(value, 'col', pairs)  9.78 us
  transfers between devices with their start and end apart: 11, of which 8 were waited for; matrix products, arithmetic and copies ran while one was open for 0% of the time, Pallas kernels for 13%

profile of v3, /device:TPU:35, one launch (start us, length us, event | category | flops | bytes accessed | tf_op | source)
XLA Modules:
  0.0 331.8 jit_solution(12629536980458727526)
XLA Ops:
  7.2 4.0 %diag.1 = f32[8,16,576]{2,1,0:T(8,128)} custom-call(s32[2,64]{1,0:T(2,128)} %bitcast.10, f32[64,2,16,576]{3,2,1,0:T(8,128)} %factors_ref.9, f32[1,576]{1,0:T(1,128)} %damping_ref.1, f32[1,576]{1,0:T(1,128)} %rhs_ref.1), custom_call_target="tpu_custom_call" | custom-call | tf_op jit(solution)/shard_map/diag/pallas_call | solution.py:381
  11.2 12.7 %all_to_all.35.in_ref = f32[8,16,576]{2,1,0:T(8,128)} all-to-all(f32[8,16,576]{2,1,0:T(8,128)} %diag.1), channel_id=1, replica_groups=mesh['row'=8,'col'=8,'track'=4] {'row'}, dimensions={0} | all-to-all | bytes 589824 | tf_op jit(solution)/shard_map/all_to_all | solution.py:27
  25.5 4.3 %all-to-all-start.1 = ((f32[4,8,576]{2,1,0:T(8,128)}), f32[4,8,576]{2,1,0:T(8,128)S(1)}, u32[]{:S(2)}, u32[]{:S(2)}) async-start(f32[4,8,576]{2,1,0:T(8,128)} %get-tuple-element.22), calls=%async_computation.1 | async-start | bytes 163840 | tf_op jit(solution)/shard_map/all_to_all | solution.py:27
  29.8 11.6 %pack.3 = f32[32,5,16,1152]{3,2,1,0:T(8,128)} custom-call(s32[2,64]{1,0:T(2,128)} %bitcast.11, s32[64]{0:T(128)} %flip_ref.3, f32[64,2,16,576]{3,2,1,0:T(8,128)} %factors_ref.9), custom_call_target="tpu_custom_call" | custom-call | bytes 16515072 | tf_op jit(solution)/shard_map/pack/pallas_call | solution.py:116
  43.5 6.4 %all-to-all-start.3 = ((f32[32,5,16,1152]{3,2,1,0:T(8,128)}), f32[32,5,16,1152]{3,2,1,0:T(8,128)}, u32[]{:S(2)}, u32[]{:S(2)}) async-start(f32[32,5,16,1152]{3,2,1,0:T(8,128)} %pack.3), calls=%async_computation.3 | async-start | bytes 23592960 | tf_op jit(solution)/shard_map/all_to_all | solution.py:27
  50.1 2.9 collective-permute-done
  53.0 3.2 collective-permute-start.1
  57.8 5.3 %collective-permute-start.2 = (f32[8,576]{1,0:T(8,128)S(1)}, f32[8,576]{1,0:T(8,128)S(1)}, u32[]{:S(2)}, u32[]{:S(2)}) collective-permute-start(f32[8,576]{1,0:T(8,128)S(1)} %add.21), channel_id=1, source_target_pairs={{0,16},{4,20},{8,24},{12,28},{16,0},{20,4},{24,8},{28,12},{1,17},{... | collective-permute-start | bytes 55304 | tf_op jit(solution)/shard_map/ppermute | solution.py:54
  64.9 4.5 %begin.1 = (f32[8,576]{1,0:T(8,128)}, f32[5,8,576]{2,1,0:T(8,128)}) custom-call(s32[2,64]{1,0:T(2,128)} %bitcast.12, f32[64,2,16,576]{3,2,1,0:T(8,128)} %factors_ref.9, f32[2,8,576]{2,1,0:T(8,128)} %get-tuple-element.21.vectors_ref, f32[8,576]{1,0:T(8,128)} %add.22.diag_ref), custom_call_target="tpu_custom_call" | custom-call | tf_op jit(solution)/shard_map/begin/pallas_call | solution.py:401
  70.2 2.5 collective-permute-done.3
  73.4 2.5 collective-permute-start.4
  77.5 5.2 %collective-permute-start.5 = (f32[8,576]{1,0:T(8,128)S(1)}, f32[8,576]{1,0:T(8,128)S(1)}, u32[]{:S(2)}, u32[]{:S(2)}) collective-permute-start(f32[8,576]{1,0:T(8,128)S(1)} %add.24), channel_id=1, source_target_pairs={{0,16},{4,20},{8,24},{12,28},{16,0},{20,4},{24,8},{28,12},{1,17},{... | collective-permute-start | bytes 55304 | tf_op jit(solution)/shard_map/ppermute | solution.py:54
  82.7 6.6 %pack.2 = f32[32,1,16,1152]{3,2,1,0:T(8,128)} custom-call(s32[2,64]{1,0:T(2,128)} %bitcast.13, s32[64]{0:T(128)} %flip_ref.3, f32[64,2,16,576]{3,2,1,0:T(8,128)} %factors_ref.9), custom_call_target="tpu_custom_call" | custom-call | bytes 7077888 | tf_op jit(solution)/shard_map/pack/pallas_call | solution.py:116
  89.4 112.1 %all-to-all-done.3.in_ref = f32[32,5,16,1152]{3,2,1,0:T(8,128)} async-done(((f32[32,5,16,1152]{3,2,1,0:T(8,128)}), f32[32,5,16,1152]{3,2,1,0:T(8,128)}, u32[]{:S(2)}, u32[]{:S(2)}) %all-to-all-start.3) | async-done | bytes 11796512 | tf_op jit(solution)/shard_map/all_to_all | solution.py:27
  201.4 6.9 %all-to-all-start.2 = ((f32[32,1,16,1152]{3,2,1,0:T(8,128)}), f32[32,1,16,1152]{3,2,1,0:T(8,128)S(1)}, u32[]{:S(2)}, u32[]{:S(2)}) async-start(f32[32,1,16,1152]{3,2,1,0:T(8,128)} %pack.2), calls=%async_computation.2 | async-start | bytes 4718592 | tf_op jit(solution)/shard_map/all_to_all | solution.py:27
  208.4 13.1 %early.1.blocks_ref = f32[8,144,576]{2,1,0:T(8,128)} custom-call(s32[1]{0:T(128)} %bitcast.3.track_ref, f32[32,5,16,1152]{3,2,1,0:T(8,128)} %all-to-all-done.3.in_ref), custom_call_target="tpu_custom_call" | custom-call | flops 6291456000 | bytes 14450688 | tf_op jit(solution)/shard_map/early/pallas_call | solution.py:216
  221.5 16.1 %all-to-all-done.2.in_ref = f32[32,1,16,1152]{3,2,1,0:T(8,128)S(1)} async-done(((f32[32,1,16,1152]{3,2,1,0:T(8,128)}), f32[32,1,16,1152]{3,2,1,0:T(8,128)S(1)}, u32[]{:S(2)}, u32[]{:S(2)}) %all-to-all-start.2) | async-done | bytes 2359328 | tf_op jit(solution)/shard_map/all_to_all | solution.py:27
  239.0 5.9 %late.1 = f32[8,144,576]{2,1,0:T(8,128)} custom-call(s32[1]{0:T(128)} %bitcast.3.track_ref, f32[32,1,16,1152]{3,2,1,0:T(8,128)} %copy-done, f32[8,144,576]{2,1,0:T(8,128)} %early.1.blocks_ref), custom_call_target="tpu_custom_call" | custom-call | flops 1258291200 | bytes 5013504 | tf_op jit(solution)/shard_map/late/pallas_call | solution.py:233
  245.0 17.3 %all_to_all.36.images_ref = f32[32,8,576]{2,1,0:T(8,128)} all-to-all(f32[32,8,576]{2,1,0:T(8,128)S(1)} %broadcast_in_dim.4), channel_id=1, replica_groups=mesh['row'=8,'col'=8,'track'=4] {'row','track'}, dimensions={0} | all-to-all | bytes 1179648 | tf_op jit(solution)/shard_map/all_to_all | solution.py:27
  262.3 5.2 %iterate.1 = (f32[32,2,576]{2,1,0:T(2,128)}, f32[5,8,576]{2,1,0:T(8,128)}) custom-call(s32[2,64]{1,0:T(2,128)} %bitcast.14, f32[64,2,16,576]{3,2,1,0:T(8,128)} %factors_ref.9, f32[5,8,576]{2,1,0:T(8,128)} %get-tuple-element.26.state_ref, f32[32,8,576]{2,1,0:T(8,128)} %all_to_all.36.images_ref), custom_call_target="tpu_custom_call" | custom-call | tf_op jit(solution)/shard_map/iterate/pallas_call | solution.py:420
  267.5 12.9 %all_to_all.37.in_ref = f32[32,2,576]{2,1,0:T(2,128)} all-to-all(f32[32,2,576]{2,1,0:T(2,128)} %get-tuple-element.34), channel_id=1, replica_groups=mesh['row'=8,'col'=8,'track'=4] {'row','track'}, dimensions={0} | all-to-all | bytes 294912 | tf_op jit(solution)/shard_map/all_to_all | solution.py:27
  282.0 14.1 %all_to_all.38.images_ref = f32[8,2,576]{2,1,0:T(2,128)} all-to-all(f32[8,2,576]{2,1,0:T(2,128)} %relay.3), channel_id=1, replica_groups=mesh['row'=8,'col'=8,'track'=4] {'col'}, dimensions={0} | all-to-all | bytes 73728 | tf_op jit(solution)/shard_map/all_to_all | solution.py:27
  296.1 2.0 collective-permute-start.6
  299.8 24.4 %collective-permute-done.6 = f32[144,576]{1,0:T(8,128)S(1)} collective-permute-done((f32[144,576]{1,0:T(8,128)}, f32[144,576]{1,0:T(8,128)S(1)}, u32[]{:S(2)}, u32[]{:S(2)}) %collective-permute-start.6) | collective-permute-done | bytes 331808 | tf_op jit(solution)/shard_map/ppermute | solution.py:439
  (28 shorter events, 16.0 us)
Async XLA Ops:
  25.5 15.9 %all-to-all-start.1 = ((f32[4,8,576]{2,1,0:T(8,128)}), f32[4,8,576]{2,1,0:T(8,128)S(1)}, u32[]{:S(2)}, u32[]{:S(2)}) async-start(f32[4,8,576]{2,1,0:T(8,128)} %get-tuple-element.22), calls=%async_computation.1 | async-start | bytes 163840 | tf_op jit(solution)/shard_map/all_to_all | solution.py:27
  41.4 0.6 copy-start.1
  43.5 6.4 %copy-start.2 = (f32[1,8,576]{2,1,0:T(8,128)S(1)}, f32[1,8,576]{2,1,0:T(8,128)}, u32[]{:S(2)}) copy-start(f32[1,8,576]{2,1,0:T(8,128)} %relay.2) | copy-start | bytes 55300
  43.5 158.0 %all-to-all-start.3 = ((f32[32,5,16,1152]{3,2,1,0:T(8,128)}), f32[32,5,16,1152]{3,2,1,0:T(8,128)}, u32[]{:S(2)}, u32[]{:S(2)}) async-start(f32[32,5,16,1152]{3,2,1,0:T(8,128)} %pack.3), calls=%async_computation.3 | async-start | bytes 23592960 | tf_op jit(solution)/shard_map/all_to_all | solution.py:27
  49.9 3.1 collective-permute-start
  53.0 4.8 %collective-permute-start.1 = (f32[8,576]{1,0:T(8,128)S(1)}, f32[8,576]{1,0:T(8,128)S(1)}, u32[]{:S(2)}, u32[]{:S(2)}) collective-permute-start(f32[8,576]{1,0:T(8,128)S(1)} %add.20), channel_id=1, source_target_pairs={{0,8},{4,12},{8,0},{12,4},{16,24},{20,28},{24,16},{28,20},{1,9},{5... | collective-permute-start | bytes 55304 | tf_op jit(solution)/shard_map/ppermute | solution.py:54
  57.8 6.5 %collective-permute-start.2 = (f32[8,576]{1,0:T(8,128)S(1)}, f32[8,576]{1,0:T(8,128)S(1)}, u32[]{:S(2)}, u32[]{:S(2)}) collective-permute-start(f32[8,576]{1,0:T(8,128)S(1)} %add.21), channel_id=1, source_target_pairs={{0,16},{4,20},{8,24},{12,28},{16,0},{20,4},{24,8},{28,12},{1,17},{... | collective-permute-start | bytes 55304 | tf_op jit(solution)/shard_map/ppermute | solution.py:54
  69.5 3.2 collective-permute-start.3
  73.4 4.0 %collective-permute-start.4 = (f32[8,576]{1,0:T(8,128)S(1)}, f32[8,576]{1,0:T(8,128)S(1)}, u32[]{:S(2)}, u32[]{:S(2)}) collective-permute-start(f32[8,576]{1,0:T(8,128)S(1)} %add.23), channel_id=1, source_target_pairs={{0,8},{4,12},{8,0},{12,4},{16,24},{20,28},{24,16},{28,20},{1,9},{5... | collective-permute-start | bytes 55304 | tf_op jit(solution)/shard_map/ppermute | solution.py:54
  77.5 11.8 %collective-permute-start.5 = (f32[8,576]{1,0:T(8,128)S(1)}, f32[8,576]{1,0:T(8,128)S(1)}, u32[]{:S(2)}, u32[]{:S(2)}) collective-permute-start(f32[8,576]{1,0:T(8,128)S(1)} %add.24), channel_id=1, source_target_pairs={{0,16},{4,20},{8,24},{12,28},{16,0},{20,4},{24,8},{28,12},{1,17},{... | collective-permute-start | bytes 55304 | tf_op jit(solution)/shard_map/ppermute | solution.py:54
  201.4 36.1 %all-to-all-start.2 = ((f32[32,1,16,1152]{3,2,1,0:T(8,128)}), f32[32,1,16,1152]{3,2,1,0:T(8,128)S(1)}, u32[]{:S(2)}, u32[]{:S(2)}) async-start(f32[32,1,16,1152]{3,2,1,0:T(8,128)} %pack.2), calls=%async_computation.2 | async-start | bytes 4718592 | tf_op jit(solution)/shard_map/all_to_all | solution.py:27
  208.4 87.7 %reduce-scatter.2.cloned.1.call-start = ((), (), s32[]{:S(2)}) async-start(), calls=%async_computation.8 | async-start | bytes 3317760 | tf_op jit(solution)/shard_map/reduce_scatter | solution.py:418
  237.5 1.5 copy-start
  296.1 28.1 %collective-permute-start.6 = (f32[144,576]{1,0:T(8,128)}, f32[144,576]{1,0:T(8,128)S(1)}, u32[]{:S(2)}, u32[]{:S(2)}) collective-permute-start(f32[144,576]{1,0:T(8,128)} %reduce-scatter.2.cloned.1.call-done), channel_id=1, source_target_pairs={{0,0},{28,1},{24,2},{20,3},{9,8},{5,9},{1,10},{29,11},{18,16},{14,... | collective-permute-start | bytes 995336 | tf_op jit(solution)/shard_map/ppermute | solution.py:439
Sparse Core Ops, SparseCore 0:
  245.1 42.2 reduce-scatter.1
